TPU v7x, 32 devices: a whole 2x2x4 slice. The times are simulated.
32 devices in a mesh: groups: 2 (over y), dp: 2 (over core), seq: 8 (over z, x).
Axes of the slice: x: 2, y: 2, z: 4, core: 2. Of those that a mesh axis runs over, the one named last changes fastest.
Arguments:
- query_proj: bfloat16 [4, 1024, 2048], P(('groups', 'dp'), 'seq'), parts along dimension 0, may hold values from -6 to 6
- key_proj: bfloat16 [4, 1024, 2048], P(('groups', 'dp'), 'seq'), parts along dimension 0, may hold values from -6 to 6
- value_proj: bfloat16 [4, 1024, 2048], P(('groups', 'dp'), 'seq'), parts along dimension 0, may hold values from -6 to 6
- cotangent: bfloat16 [4, 1024, 2048], P(('groups', 'dp'), 'seq'), parts along dimension 0, may hold values from -6 to 6
- boundary: int32 [4], P(('groups', 'dp')), parts along dimension 0, may hold values from 128 to 511
- short_taps: float32 [3, 3, 2048], replicated, may hold values from -3 to 3
- skip_gain: float32 [2048], replicated, may hold values from -4 to 4
- long_filter: bfloat16 [1024, 2048], P('seq'), may hold values from -1.1 to 1.1
Outputs:
- query_grad: bfloat16 [4, 1024, 2048], P(('groups', 'dp'), 'seq'), parts along dimension 0
- key_grad: bfloat16 [4, 1024, 2048], P(('groups', 'dp'), 'seq'), parts along dimension 0
- value_grad: bfloat16 [4, 1024, 2048], P(('groups', 'dp'), 'seq'), parts along dimension 0
- filter_grad: bfloat16 [2048, 2048], P(('groups', 'seq')), parts along dimension 0
- taps_grad: float32 [6, 3, 2048], P('groups', None, 'seq'), parts along dimension 0
- skip_grad: float32 [4096], P(('groups', 'seq')), parts along dimension 0
There are 2 independent parts, one for each index of `groups`. A program takes and returns all parts, laid end to end along the dimension named above; an argument that names none is the same for every part. Nothing has to cross between parts.
All inputs are finite; a program needn't handle non-finite values.
Results may differ from a plain program's by a relative error of at most 0.001.
Values may be sent and summed in bfloat16 or wider, within the bound.
A program may use at most 128 MiB of HBM per device.

v0:
```python
import math

import jax
import jax.numpy as jnp
from jax import lax
from jax.sharding import PartitionSpec as P


def passed_along(value, axis, by):
    count = lax.axis_size(axis)
    pairs = [(i, i + by) for i in range(count) if 0 <= i + by < count]
    return lax.ppermute(value, axis, pairs)


def matmul_high(form, left, right):
    return jnp.einsum(
        form, left, right, precision=lax.Precision.HIGHEST, preferred_element_type=jnp.float32
    )


def dot_high(left, right):
    return jnp.dot(left, right, precision=lax.Precision.HIGHEST, preferred_element_type=jnp.float32)


def angle_table(left, right, period):
    phase = (left[:, None] * right[None, :] % period).astype(jnp.float32) * (2.0 * math.pi / period)
    return (jnp.cos(phase), jnp.sin(phase))


def build_tables(seq_len):
    cols = min(128, seq_len)
    rows = 2 * seq_len // cols
    half = rows // 2
    keep = half + 1
    col_index = jnp.arange(cols, dtype=jnp.int32)
    keep_index = jnp.arange(keep, dtype=jnp.int32)
    half_index = jnp.arange(half, dtype=jnp.int32)
    col_cos, col_sin = angle_table(col_index, col_index, cols)
    first_cos, first_sin = angle_table(keep_index, half_index, rows)
    first = jnp.stack((first_cos, -first_sin))
    twist_cos, twist_sin = angle_table(keep_index, col_index, 2 * seq_len)
    twist_cos = twist_cos[:, None, :]
    twist_sin = twist_sin[:, None, :]
    fwd_real = jnp.concatenate((col_cos, -col_sin), axis=1)
    fwd_imag = jnp.concatenate((col_sin, col_cos), axis=1)
    inv_real = jnp.concatenate((col_cos, col_sin), axis=1)
    inv_imag = jnp.concatenate((-col_sin, col_cos), axis=1)
    edge = (keep_index == 0) | (keep_index == half)
    weights = jnp.where(edge, 1.0, 2.0).astype(jnp.float32) / (2.0 * seq_len)
    last_cos, last_sin = angle_table(half_index, keep_index, rows)
    last_cos = last_cos * weights[None, :]
    last_sin = last_sin * weights[None, :]
    return (first, twist_cos, twist_sin, fwd_real, fwd_imag, inv_real, inv_imag, last_cos, last_sin)


def forward_half(signal, tables):
    first, twist_cos, twist_sin, fwd_real, fwd_imag = tables[:5]
    width_c, length = signal.shape
    cols = fwd_real.shape[0]
    grid = jnp.transpose(signal.reshape(width_c, length // cols, cols), (1, 0, 2))
    partial_dft = matmul_high("pkn,nca->pkca", first, grid)
    turned_re = partial_dft[0] * twist_cos + partial_dft[1] * twist_sin
    turned_im = partial_dft[1] * twist_cos - partial_dft[0] * twist_sin
    keep = partial_dft.shape[1]
    spec = dot_high(turned_re.reshape(-1, cols), fwd_real) + dot_high(
        turned_im.reshape(-1, cols), fwd_imag
    )
    spec = spec.reshape(keep, width_c, 2, cols)
    return (spec[:, :, 0], spec[:, :, 1])


def inverse_half(spec_re, spec_im, tables):
    twist_cos, twist_sin = (tables[1], tables[2])
    inv_real, inv_imag, last_cos, last_sin = tables[5:]
    keep, width_c, cols = spec_re.shape
    wide = dot_high(spec_re.reshape(-1, cols), inv_real) + dot_high(
        spec_im.reshape(-1, cols), inv_imag
    )
    wide = wide.reshape(keep, width_c, 2, cols)
    wide_re = wide[:, :, 0]
    wide_im = wide[:, :, 1]
    turned_re = wide_re * twist_cos - wide_im * twist_sin
    turned_im = wide_im * twist_cos + wide_re * twist_sin
    grid = matmul_high("nk,kca->nca", last_cos, turned_re) - matmul_high(
        "nk,kca->nca", last_sin, turned_im
    )
    return jnp.transpose(grid, (1, 0, 2)).reshape(width_c, -1)


def convolve_cols(gated_spec, filt_spec, tables):
    gated_re, gated_im = gated_spec
    filt_re, filt_im = filt_spec
    return inverse_half(
        gated_re * filt_re - gated_im * filt_im, gated_re * filt_im + gated_im * filt_re, tables
    )


def correlate_cols(gated_spec, filt_spec, dmix_cols, tables):
    gated_re, gated_im = gated_spec
    filt_re, filt_im = filt_spec
    grad_re, grad_im = forward_half(dmix_cols, tables)
    back = inverse_half(
        filt_re * grad_re + filt_im * grad_im, filt_re * grad_im - filt_im * grad_re, tables
    )
    filt_part = inverse_half(
        grad_re * gated_re + grad_im * gated_im, grad_im * gated_re - grad_re * gated_im, tables
    )
    return (back, filt_part)


def body(query_proj, key_proj, value_proj, cotangent, boundary, short_taps, skip_gain, long_filter):
    pairs, tok, width = query_proj.shape
    parts = lax.axis_size("seq")
    seq_len = tok * parts
    scale = 1.0 / math.sqrt(pairs * lax.axis_size("dp") * seq_len)
    tables = build_tables(seq_len)
    filter_cols = lax.all_to_all(
        jnp.transpose(long_filter), "seq", split_axis=0, concat_axis=1, tiled=True
    ).astype(jnp.float32)
    filt_spec = forward_half(filter_cols, tables)
    taps = short_taps[:, :, None, None, :]
    raw = jnp.stack((query_proj, key_proj, value_proj))
    tails = passed_along(raw[:, :, tok - 2 :], "seq", 1)
    extended = jnp.concatenate((tails, raw), axis=2).astype(jnp.float32)
    conv = (
        taps[:, 0] * extended[:, :, 2:]
        + taps[:, 1] * extended[:, :, 1:-1]
        + taps[:, 2] * extended[:, :, :-2]
    )
    gated = conv[1] * conv[2]
    position = lax.axis_index("seq") * tok + jnp.arange(tok, dtype=jnp.int32)
    mask = (position[None, :] >= boundary[:, None]).astype(jnp.float32)
    dout = cotangent.astype(jnp.float32) * mask[:, :, None]
    dmix = dout * conv[0]
    gated_cols = lax.all_to_all(
        jnp.transpose(gated, (0, 2, 1)), "seq", split_axis=1, concat_axis=2, tiled=True
    )
    spectra = forward_half(gated_cols[0], tables)
    conv_cols = jnp.stack([convolve_cols(spectra, filt_spec, tables)])
    conv_rows = lax.all_to_all(conv_cols, "seq", split_axis=2, concat_axis=1, tiled=True)
    dmix_cols = lax.all_to_all(
        jnp.transpose(dmix, (0, 2, 1)), "seq", split_axis=1, concat_axis=2, tiled=True
    )
    back_cols, filt_part = correlate_cols(spectra, filt_spec, dmix_cols[0], tables)
    back_list = [back_cols]
    filt_list = [filt_part]
    back_rows = lax.all_to_all(jnp.stack(back_list), "seq", split_axis=2, concat_axis=1, tiled=True)
    mixed = jnp.transpose(conv_rows, (0, 2, 1)) + skip_gain * gated
    filter_part = jnp.sum(jnp.stack(filt_list), axis=0) * scale
    filter_total = lax.psum(filter_part, "dp")
    filter_rows = lax.all_to_all(
        filter_total.astype(jnp.bfloat16), "seq", split_axis=1, concat_axis=0, tiled=True
    )
    filter_grad = jnp.transpose(filter_rows)
    dgated = jnp.transpose(back_rows, (0, 2, 1)) + skip_gain * dmix
    upstream = jnp.stack((dout * mixed, dgated * conv[2], dgated * conv[1]))
    heads = passed_along(upstream[:, :, :2], "seq", -1)
    grad_ext = jnp.concatenate((upstream, heads), axis=2)
    grads = (
        taps[:, 0] * grad_ext[:, :, :tok]
        + taps[:, 1] * grad_ext[:, :, 1 : tok + 1]
        + taps[:, 2] * grad_ext[:, :, 2:]
    )
    grads = grads.astype(jnp.bfloat16)
    taps_part = (
        jnp.stack(
            [
                jnp.sum(upstream * extended[:, :, 2 - lag : 2 - lag + tok], axis=(1, 2))
                for lag in range(3)
            ],
            axis=1,
        )
        * scale
    )
    skip_part = jnp.sum(dmix * gated, axis=(0, 1)) * scale
    taps_local, skip_local = (
        lax.psum_scatter(taps_part, "seq", scatter_dimension=2, tiled=True),
        lax.psum_scatter(skip_part, "seq", scatter_dimension=0, tiled=True),
    )
    taps_grad, skip_grad = lax.psum((taps_local, skip_local), "dp")
    return (grads[0], grads[1], grads[2], filter_grad, taps_grad, skip_grad)


def solution(mesh):
    in_specs = (
        P(("groups", "dp"), "seq", None),
        P(("groups", "dp"), "seq", None),
        P(("groups", "dp"), "seq", None),
        P(("groups", "dp"), "seq", None),
        P(("groups", "dp")),
        P(),
        P(),
        P("seq", None),
    )
    out_specs = (
        P(("groups", "dp"), "seq", None),
        P(("groups", "dp"), "seq", None),
        P(("groups", "dp"), "seq", None),
        P(("groups", "seq"), None),
        P("groups", None, "seq"),
        P(("groups", "seq")),
    )
    return jax.shard_map(body, mesh=mesh, in_specs=in_specs, out_specs=out_specs, check_vma=False)
```

profile of v0, /device:TPU:0, one launch (start us, length us, event | category | flops | bytes accessed | tf_op | source)
XLA Modules:
  0.0 408.0 jit_solution(7509507774714308485)
XLA Ops:
  8.1 5.0 %collective-permute-start = (bf16[3,1,2,2048]{3,2,1,0:T(2,128)(2,1)S(1)}, bf16[3,1,2,2048]{3,2,1,0:T(2,128)(2,1)S(1)}, u32[]{:S(2)}, u32[]{:S(2)}) collective-permute-start(bf16[3,1,2,2048]{3,2,1,0:T(2,128)(2,1)S(1)} %pad_maximum_fusion.18), channel_id=1, source_target_pairs={{0,1},{1,2},{2,3},{3,4},{4,5},{5,6},{6,7},{8,9},{9,10},{10,11},{11... | collective-permute-start | bytes 73736 | tf_op jit(solution)/shard_map/ppermute | solution.py:12
  14.1 4.9 %all-to-all-start.1 = ((bf16[8,256,128]{2,1,0:T(8,128)(2,1)}), bf16[8,256,128]{2,1,0:T(8,128)(2,1)}, u32[]{:S(2)}, u32[]{:S(2)}) async-start(bf16[8,256,128]{2,1,0:T(8,128)(2,1)} %bitcast.22), calls=%async_computation.1 | async-start | bytes 1048576 | tf_op jit(solution)/shard_map/all_to_all | solution.py:117
  19.8 1.9 maximum_convert_fusion
  22.7 2.6 multiply_reduce_fusion.3
  25.3 3.6 copy.86
  28.9 4.4 %all-to-all-done.1 = bf16[8,256,128]{2,1,0:T(8,128)(2,1)} async-done(((bf16[8,256,128]{2,1,0:T(8,128)(2,1)}), bf16[8,256,128]{2,1,0:T(8,128)(2,1)}, u32[]{:S(2)}, u32[]{:S(2)}) %all-to-all-start.1) | async-done | bytes 524320 | tf_op jit(solution)/shard_map/all_to_all | solution.py:117
  33.3 4.2 %all-to-all-start = ((f32[1,2048,128]{2,0,1:T(1,128)}), f32[1,2048,128]{2,0,1:T(1,128)}, u32[]{:S(2)}, u32[]{:S(2)}) async-start(f32[1,2048,128]{2,0,1:T(1,128)} %copy.86), calls=%async_computation | async-start | bytes 2097152 | tf_op jit(solution)/shard_map/all_to_all | solution.py:135
  38.2 3.6 copy.100
  41.8 21.2 %all-to-all-done = f32[1,2048,128]{2,0,1:T(1,128)} async-done(((f32[1,2048,128]{2,0,1:T(1,128)}), f32[1,2048,128]{2,0,1:T(1,128)}, u32[]{:S(2)}, u32[]{:S(2)}) %all-to-all-start) | async-done | bytes 1048608 | tf_op jit(solution)/shard_map/all_to_all | solution.py:135
  63.0 4.7 %all-to-all-start.3 = ((f32[1,2048,128]{2,0,1:T(1,128)}), f32[1,2048,128]{2,0,1:T(1,128)}, u32[]{:S(2)}, u32[]{:S(2)}) async-start(f32[1,2048,128]{2,0,1:T(1,128)} %copy.100), calls=%async_computation.3 | async-start | bytes 2097152 | tf_op jit(solution)/shard_map/all_to_all | solution.py:141
  68.9 2.9 fusion.49
  74.9 4.8 %fusion.42 = f32[2,9,256,128]{3,1,2,0:T(8,128)S(1)} fusion(f32[1,8,256,128]{3,2,1,0:T(8,128)} %bitcast.11, f32[1,9,8]{1,2,0:T(8,128)S(1)} %copy-done.31, f32[1,9,8]{1,2,0:T(8,128)S(1)} %copy-done.32), kind=kOutput, calls=%fused_computation.73 | convolution fusion | flops 56623248 | bytes 3408448 | tf_op jit(solution)/shard_map/pkn,nca->pkca/dot_general | solution.py:16
  82.7 9.9 %all-to-all-done.3 = f32[1,2048,128]{2,0,1:T(1,128)} async-done(((f32[1,2048,128]{2,0,1:T(1,128)}), f32[1,2048,128]{2,0,1:T(1,128)}, u32[]{:S(2)}, u32[]{:S(2)}) %all-to-all-start.3) | async-done | bytes 1048608 | tf_op jit(solution)/shard_map/all_to_all | solution.py:141
  92.7 4.8 %fusion.40 = f32[2,9,256,128]{3,1,2,0:T(8,128)S(1)} fusion(f32[1,8,256,128]{3,2,1,0:T(8,128)} %bitcast.38, f32[1,9,8]{1,2,0:T(8,128)} %get-tuple-element.85, f32[1,9,8]{1,2,0:T(8,128)} %get-tuple-element.86), kind=kOutput, calls=%fused_computation.71 | convolution fusion | flops 56623248 | bytes 3408448 | tf_op jit(solution)/shard_map/pkn,nca->pkca/dot_general | solution.py:16
  100.4 2.6 fusion.34
  103.0 2.0 fusion.52
  105.1 3.5 convolution_add_fusion.2
  108.6 3.8 reshape.398
  112.4 3.4 fusion.54
  115.8 3.5 convolution_add_fusion.5
  119.3 4.1 %reshape.395 = f32[9,256,2,128]{3,2,1,0:T(2,128)} reshape(f32[2304,256]{1,0:T(8,128)} %convolution_add_fusion.5) | data formatting | bytes 4718592 | tf_op jit(solution)/shard_map/reshape | solution.py:68
  123.4 3.4 fusion.53
  126.9 3.4 convolution_add_fusion.4
  130.3 3.8 reshape.396
  134.0 8.3 %multiply_subtract_fusion.3 = (f32[9,256,1,128]{3,2,1,0:T(1,128)}, f32[9,256,1,128]{3,2,1,0:T(1,128)}) fusion(f32[9,256,2,128]{3,2,1,0:T(2,128)} %reshape.398, f32[9,256,2,128]{3,2,1,0:T(2,128)} %reshape.396), kind=kLoop, calls=%fused_computation.60 | loop fusion | flops 1769472 | bytes 7077888 | tf_op jit(solution)/shard_map/sub | solution.py:103
  142.3 6.5 %multiply_subtract_fusion.1 = (f32[9,256,1,128]{3,2,1,0:T(1,128)S(1)}, f32[9,256,1,128]{3,2,1,0:T(1,128)S(1)}, f32[9,256,1,128]{3,2,1,0:T(1,128)}, f32[9,256,1,128]{3,2,1,0:T(1,128)}) fusion(f32[9,256,2,128]{3,2,1,0:T(2,128)S(1)} %copy-done.1, f32[9,256,2,128]{3,2,1,0:T(2,128)S(1)} %copy-done.3, f32[9,256,2,128]{3,2,1,0:T(2,128)S(1)} %copy-done.2), kind=kLoop, calls=%fused_computation.56 | loop fusion | flops 3538944 | bytes 11796480 | tf_op jit(solution)/shard_map/sub | solution.py:106
  148.8 2.0 fusion.55
  150.8 3.5 convolution_add_fusion
  154.3 3.9 reshape.400
  158.2 6.3 %fusion.151 = (f32[9,256,1,128]{3,2,1,0:T(1,128)}, f32[9,256,1,128]{3,2,1,0:T(1,128)}) fusion(f32[9,256,2,128]{3,2,1,0:T(2,128)} %reshape.400), kind=kLoop, calls=%fused_computation.216 | loop fusion | bytes 4718592 | tf_op jit(solution)/shard_map/slice | solution.py:81
  164.5 2.0 fusion.57
  166.6 3.5 convolution_add_fusion.3
  170.1 3.8 reshape.397
  173.8 6.3 %fusion.152 = (f32[9,256,1,128]{3,2,1,0:T(1,128)}, f32[9,256,1,128]{3,2,1,0:T(1,128)}) fusion(f32[9,256,2,128]{3,2,1,0:T(2,128)} %reshape.397), kind=kLoop, calls=%fused_computation.217 | loop fusion | bytes 4718592 | tf_op jit(solution)/shard_map/slice | solution.py:81
  180.2 2.0 fusion.56
  182.2 3.4 convolution_add_fusion.1
  185.6 4.1 %reshape.399 = f32[9,256,2,128]{3,2,1,0:T(2,128)} reshape(f32[2304,256]{1,0:T(8,128)} %convolution_add_fusion.1) | data formatting | bytes 4718592 | tf_op jit(solution)/shard_map/reshape | solution.py:79
  189.8 4.9 %fusion.153 = (f32[9,256,1,128]{3,2,1,0:T(1,128)S(1)}, f32[9,256,1,128]{3,2,1,0:T(1,128)S(1)}) fusion(f32[9,256,2,128]{3,2,1,0:T(2,128)} %reshape.399), kind=kLoop, calls=%fused_computation.218 | loop fusion | bytes 4718592 | tf_op jit(solution)/shard_map/slice | solution.py:81
  194.7 2.9 multiply_subtract_fusion
  199.4 2.8 fusion.24
  202.2 2.4 stack_reshape.8
  204.6 3.6 copy.108
  208.2 4.2 %all-to-all-start.4 = ((f32[1,256,1024]{1,0,2:T(1,128)}), f32[1,256,1024]{1,0,2:T(1,128)}, u32[]{:S(2)}, u32[]{:S(2)}) async-start(f32[1,256,1024]{1,0,2:T(1,128)} %copy.108), calls=%async_computation.4 | async-start | bytes 2097152 | tf_op jit(solution)/shard_map/all_to_all | solution.py:147
  212.4 3.1 fusion.11
  215.6 2.8 fusion.18
  218.4 2.4 stack_reshape.7
  220.8 3.6 copy.98
  224.4 13.4 %all-to-all-done.4 = f32[1,256,1024]{1,0,2:T(1,128)} async-done(((f32[1,256,1024]{1,0,2:T(1,128)}), f32[1,256,1024]{1,0,2:T(1,128)}, u32[]{:S(2)}, u32[]{:S(2)}) %all-to-all-start.4) | async-done | bytes 1048608 | tf_op jit(solution)/shard_map/all_to_all | solution.py:147
  237.8 4.3 %all-to-all-start.2 = ((f32[1,256,1024]{1,0,2:T(1,128)}), f32[1,256,1024]{1,0,2:T(1,128)}, u32[]{:S(2)}, u32[]{:S(2)}) async-start(f32[1,256,1024]{1,0,2:T(1,128)} %copy.98), calls=%async_computation.2 | async-start | bytes 2097152 | tf_op jit(solution)/shard_map/all_to_all | solution.py:140
  243.4 30.3 %all-reduce = f32[2048]{0:T(1024)S(1)} all-reduce(f32[2048]{0:T(1024)S(1)} %broadcast_multiply_fusion), channel_id=3, replica_groups=mesh['groups'=2,'dp'=2,'seq'=8] {'seq'}, use_global_device_ids=true, to_apply=%region_7.8.clone | all-reduce | flops 2048 | bytes 16384
  273.8 2.8 copy.174
  276.6 2.4 all_to_all.87
  279.0 2.8 copy.175
  281.8 2.4 all_to_all.80
  284.2 3.3 multiply_bitcast_fusion.1
  289.2 2.8 fusion.3
  291.9 2.1 collective-permute-done.1
  294.5 3.0 multiply_reduce_fusion.2
  297.6 3.1 copy.119
  300.7 5.3 %reshape.407 = f32[2048,9]{1,0:T(8,128)} reshape(f32[2048,3,3]{2,1,0:T(4,128)} %bitcast.254) | data formatting | bytes 147456
  309.3 62.5 %reduce-scatter.4.cloned.1.call-done = f32[256,9]{1,0:T(8,128)} async-done(((f32[2048,9]{1,0:T(8,128)}), f32[256,9]{1,0:T(8,128)}) %reduce-scatter.4.cloned.1.call-update) | async-done | bytes 9232
  373.0 6.4 %all-reduce.3 = (bf16[256,1024]{1,0:T(8,128)(2,1)S(1)}, f32[3,3,256]{2,0,1:T(4,128)S(1)}, f32[256]{0:T(256)}) all-reduce(f32[256,1024]{1,0:T(8,128)S(1)} %bitcast.268, f32[3,3,256]{2,0,1:T(4,128)S(1)} %copy.120, f32[256]{0:T(256)S(1)} %dynamic-slice.1), channel_id=1, replica_groups=mesh['groups'=2,'dp'=2,'seq'=8] {'dp'}, use_global_device_ids=true, to_apply=%region_0.1 | all-reduce | flops 264704 | bytes 1593344 | tf_op jit(solution)/shard_map/psum | solution.py:150
  380.4 3.7 all-to-all-start.5
  385.9 13.8 %all-to-all-done.5 = bf16[256,8,128]{0,2,1:T(8,128)(2,1)S(1)} async-done(((bf16[256,8,128]{0,2,1:T(8,128)(2,1)}), bf16[256,8,128]{0,2,1:T(8,128)(2,1)S(1)}, u32[]{:S(2)}, u32[]{:S(2)}) %all-to-all-start.5) | async-done | bytes 524320 | tf_op jit(solution)/shard_map/all_to_all | solution.py:151
  (123 shorter events, 27.0 us)
Async XLA Ops:
  7.2 5.9 %copy-start.24 = (bf16[128,2048]{1,0:T(8,128)(2,1)S(1)}, bf16[128,2048]{1,0:T(8,128)(2,1)}, u32[]{:S(2)}) copy-start(bf16[128,2048]{1,0:T(8,128)(2,1)} %param.15) | copy-start | bytes 1572868
  8.1 10.9 %copy-start.33 = (f32[3,3,2048]{2,1,0:T(4,128)S(1)}, f32[3,3,2048]{2,1,0:T(4,128)}, u32[]{:S(2)}) copy-start(f32[3,3,2048]{2,1,0:T(4,128)} %param.13) | copy-start | bytes 221188
  8.1 11.7 %collective-permute-start = (bf16[3,1,2,2048]{3,2,1,0:T(2,128)(2,1)S(1)}, bf16[3,1,2,2048]{3,2,1,0:T(2,128)(2,1)S(1)}, u32[]{:S(2)}, u32[]{:S(2)}) collective-permute-start(bf16[3,1,2,2048]{3,2,1,0:T(2,128)(2,1)S(1)} %pad_maximum_fusion.18), channel_id=1, source_target_pairs={{0,1},{1,2},{2,3},{3,4},{4,5},{5,6},{6,7},{8,9},{9,10},{10,11},{11... | collective-permute-start | bytes 73736 | tf_op jit(solution)/shard_map/ppermute | solution.py:12
  14.1 19.2 %all-to-all-start.1 = ((bf16[8,256,128]{2,1,0:T(8,128)(2,1)}), bf16[8,256,128]{2,1,0:T(8,128)(2,1)}, u32[]{:S(2)}, u32[]{:S(2)}) async-start(bf16[8,256,128]{2,1,0:T(8,128)(2,1)} %bitcast.22), calls=%async_computation.1 | async-start | bytes 1048576 | tf_op jit(solution)/shard_map/all_to_all | solution.py:117
  19.7 2.0 copy-start.25
  19.7 2.0 copy-start.27
  19.7 2.9 copy-start.37
  19.8 1.9 copy-start.29
  21.7 1.0 copy-start.23
  22.7 2.6 copy-start
  33.3 29.7 %all-to-all-start = ((f32[1,2048,128]{2,0,1:T(1,128)}), f32[1,2048,128]{2,0,1:T(1,128)}, u32[]{:S(2)}, u32[]{:S(2)}) async-start(f32[1,2048,128]{2,0,1:T(1,128)} %copy.86), calls=%async_computation | async-start | bytes 2097152 | tf_op jit(solution)/shard_map/all_to_all | solution.py:135
  63.0 29.6 %all-to-all-start.3 = ((f32[1,2048,128]{2,0,1:T(1,128)}), f32[1,2048,128]{2,0,1:T(1,128)}, u32[]{:S(2)}, u32[]{:S(2)}) async-start(f32[1,2048,128]{2,0,1:T(1,128)} %copy.100), calls=%async_computation.3 | async-start | bytes 2097152 | tf_op jit(solution)/shard_map/all_to_all | solution.py:141
  73.5 1.4 copy-start.31
  73.5 1.4 copy-start.32
  98.0 1.3 copy-start.14
  98.0 1.6 copy-start.15
  98.4 1.7 copy-start.11
  98.4 2.0 copy-start.12
  112.4 3.4 copy-start.21
  123.4 3.4 copy-start.20
  134.0 8.3 %copy-start.1 = (f32[9,256,2,128]{3,2,1,0:T(2,128)S(1)}, f32[9,256,2,128]{3,2,1,0:T(2,128)}, u32[]{:S(2)}) copy-start(f32[9,256,2,128]{3,2,1,0:T(2,128)} %reshape.398) | copy-start | bytes 7077892
  134.0 8.3 %copy-start.2 = (f32[9,256,2,128]{3,2,1,0:T(2,128)S(1)}, f32[9,256,2,128]{3,2,1,0:T(2,128)}, u32[]{:S(2)}) copy-start(f32[9,256,2,128]{3,2,1,0:T(2,128)} %reshape.396) | copy-start | bytes 7077892
  134.0 8.3 %copy-start.3 = (f32[9,256,2,128]{3,2,1,0:T(2,128)S(1)}, f32[9,256,2,128]{3,2,1,0:T(2,128)}, u32[]{:S(2)}) copy-start(f32[9,256,2,128]{3,2,1,0:T(2,128)} %reshape.395) | copy-start | bytes 7077892
  158.2 6.3 %copy-start.8 = (f32[9,256,1,128]{3,2,1,0:T(1,128)S(1)}, f32[9,256,1,128]{3,2,1,0:T(1,128)}, u32[]{:S(2)}) copy-start(f32[9,256,1,128]{3,2,1,0:T(1,128)} %get-tuple-element.63) | copy-start | bytes 3538948
  164.5 2.1 copy-start.10
  173.8 6.3 %copy-start.9 = (f32[9,256,1,128]{3,2,1,0:T(1,128)S(1)}, f32[9,256,1,128]{3,2,1,0:T(1,128)}, u32[]{:S(2)}) copy-start(f32[9,256,1,128]{3,2,1,0:T(1,128)} %get-tuple-element.37) | copy-start | bytes 3538948
  180.2 2.0 copy-start.13
  189.8 4.9 %copy-start.16 = (f32[9,256,1,128]{3,2,1,0:T(1,128)S(1)}, f32[9,256,1,128]{3,2,1,0:T(1,128)}, u32[]{:S(2)}) copy-start(f32[9,256,1,128]{3,2,1,0:T(1,128)} %get-tuple-element.61) | copy-start | bytes 3538948
  189.8 4.9 %copy-start.17 = (f32[9,256,1,128]{3,2,1,0:T(1,128)S(1)}, f32[9,256,1,128]{3,2,1,0:T(1,128)}, u32[]{:S(2)}) copy-start(f32[9,256,1,128]{3,2,1,0:T(1,128)} %get-tuple-element.62) | copy-start | bytes 3538948
  189.8 4.9 %copy-start.18 = (f32[9,256,1,128]{3,2,1,0:T(1,128)S(1)}, f32[9,256,1,128]{3,2,1,0:T(1,128)}, u32[]{:S(2)}) copy-start(f32[9,256,1,128]{3,2,1,0:T(1,128)} %get-tuple-element.65) | copy-start | bytes 3538948
  189.8 4.9 %copy-start.19 = (f32[9,256,1,128]{3,2,1,0:T(1,128)S(1)}, f32[9,256,1,128]{3,2,1,0:T(1,128)}, u32[]{:S(2)}) copy-start(f32[9,256,1,128]{3,2,1,0:T(1,128)} %get-tuple-element.66) | copy-start | bytes 3538948
  194.7 3.0 copy-start.35
  208.2 29.7 %all-to-all-start.4 = ((f32[1,256,1024]{1,0,2:T(1,128)}), f32[1,256,1024]{1,0,2:T(1,128)}, u32[]{:S(2)}, u32[]{:S(2)}) async-start(f32[1,256,1024]{1,0,2:T(1,128)} %copy.108), calls=%async_computation.4 | async-start | bytes 2097152 | tf_op jit(solution)/shard_map/all_to_all | solution.py:147
  212.4 3.1 copy-start.6
  224.4 17.7 %copy-start.39 = (u32[32]{0:T(128)S(1)}, u32[32]{0:T(128)}, u32[]{:S(2)}) copy-start(u32[32]{0:T(128)} %constant.85) | copy-start | bytes 388
  224.4 19.0 %copy-start.34 = (f32[2048]{0:T(1024)S(1)}, f32[2048]{0:T(1024)}, u32[]{:S(2)}) copy-start(f32[2048]{0:T(1024)} %get-tuple-element.45) | copy-start | bytes 24580
  237.8 41.2 %all-to-all-start.2 = ((f32[1,256,1024]{1,0,2:T(1,128)}), f32[1,256,1024]{1,0,2:T(1,128)}, u32[]{:S(2)}, u32[]{:S(2)}) async-start(f32[1,256,1024]{1,0,2:T(1,128)} %copy.98), calls=%async_computation.2 | async-start | bytes 2097152 | tf_op jit(solution)/shard_map/all_to_all | solution.py:140
  242.1 129.6 %reduce-scatter.4.cloned.1.call-start = ((), (), s32[]{:S(2)}) async-start(), calls=%async_computation.7 | async-start | bytes 1179648
  281.8 2.4 copy-start.36
  281.8 2.4 copy-start.38
  287.5 1.7 copy-start.5
  287.9 6.2 %collective-permute-start.1 = (f32[3,1,2,2048]{3,2,1,0:T(2,128)S(1)}, f32[3,1,2,2048]{3,2,1,0:T(2,128)S(1)}, u32[]{:S(2)}, u32[]{:S(2)}) collective-permute-start(f32[3,1,2,2048]{3,2,1,0:T(2,128)S(1)} %slice.175), channel_id=1, source_target_pairs={{1,0},{2,1},{3,2},{4,3},{5,4},{6,5},{7,6},{9,8},{10,9},{11,10},{12... | collective-permute-start | bytes 147464 | tf_op jit(solution)/shard_map/ppermute | solution.py:12
  291.9 2.5 copy-start.26
  291.9 2.6 copy-start.28
  291.9 2.6 copy-start.30
  300.7 5.4 %copy-start.4 = (f32[9,256,128]{2,1,0:T(8,128)S(1)}, f32[9,256,128]{2,1,0:T(8,128)}, u32[]{:S(2)}) copy-start(f32[9,256,128]{2,1,0:T(8,128)} %get-tuple-element.49) | copy-start | bytes 3538948
  306.0 1.2 copy-start.22
  379.4 4.7 %copy-start.7 = (bf16[3,1,128,2048]{3,2,1,0:T(8,128)(2,1)S(1)}, bf16[3,1,128,2048]{3,2,1,0:T(8,128)(2,1)}, u32[]{:S(2)}) copy-start(bf16[3,1,128,2048]{3,2,1,0:T(8,128)(2,1)} %get-tuple-element.48) | copy-start | bytes 4718596
  380.4 19.3 %all-to-all-start.5 = ((bf16[256,8,128]{0,2,1:T(8,128)(2,1)}), bf16[256,8,128]{0,2,1:T(8,128)(2,1)S(1)}, u32[]{:S(2)}, u32[]{:S(2)}) async-start(bf16[256,8,128]{0,2,1:T(8,128)(2,1)} %bitcast.63), calls=%async_computation.5 | async-start | bytes 1048576 | tf_op jit(solution)/shard_map/all_to_all | solution.py:151
Sparse Core Ops, SparseCore 0:
  306.2 65.5 reduce-scatter.3
where the time goes:
time: 413 us; the launch traced here: 408 us
  waiting for transfers between devices  127 us (31%)
  local copies, waits for them, and re-layouts  96.7 us (23%)
  matrix products  63.3 us (15%)
  blocking collectives  36.7 us (9%)
  other arithmetic  35.4 us (9%)
  starting transfers between devices  32.3 us (8%)
  between operations  16.3 us (4%)
    unnamed x2, waiting for transfers between devices  62.5 us
    dot_general x12, matrix products, dot_high(): jnp.dot(left, right, precision=lax.Precision.HIGHEST, preferred_element_t...  35.8 us
    unnamed x1, blocking collectives  30.3 us
    dot_general x9, matrix products, matmul_high(): jnp.einsum(form, left, right, precision=lax.Precision.HIGHEST, preferred_...  27.6 us
    all_to_all x1, waiting for transfers between devices, body(): lax.all_to_all(jnp.transpose(gated, (0, 2, 1)), 'seq', split_axis=1, conc...  21.2 us
    slice x3, local copies, waits for them, and re-layouts, inverse_half(): wide_im = wide[:, :, 1]  17.4 us
    unnamed x92, local copies, waits for them, and re-layouts  16.3 us
    all_to_all x1, waiting for transfers between devices, body(): lax.all_to_all(filter_total.astype(jnp.bfloat16), 'seq', split_axis=1, co...  13.8 us
  transfers between devices with their start and end apart: 9, of which 7 were waited for; matrix products, arithmetic and copies ran while one was open for 13% of the time, Pallas kernels for 0%

commit v1 on v0

--- a/solution.py
+++ b/solution.py
@@ -1,9 +1,15 @@
+import functools
 import math
 
 import jax
 import jax.numpy as jnp
+import numpy as np
 from jax import lax
+from jax.experimental import pallas as pl
+from jax.experimental.pallas import tpu as pltpu
 from jax.sharding import PartitionSpec as P
+
+DENSE_LIMIT = 2048
 
 
 def passed_along(value, axis, by):
@@ -108,6 +114,194 @@
     return (back, filt_part)
 
 
+def dense_tables(n):
+    index = 4 * np.arange(n, dtype=np.int64) + 1
+    phase = (index[:, None] * index[None, :] % (16 * n)) * (2.0 * np.pi / (16 * n))
+    parts = []
+    for table in (np.cos(phase), np.sin(phase)):
+        high = table.astype(jnp.bfloat16)
+        parts.append(high)
+        parts.append((table - high.astype(np.float64)).astype(jnp.bfloat16))
+    turn = index * (2.0 * np.pi / (16 * n))
+    twist = np.stack((np.cos(turn), np.sin(turn)))[:, :, None].astype(np.float32)
+    return tuple(parts), twist
+
+
+def split_to(ref, lead, rows, value):
+    high = value.astype(jnp.bfloat16)
+    ref[(*lead, 0, rows)] = high
+    ref[(*lead, 1, rows)] = (value - high.astype(jnp.float32)).astype(jnp.bfloat16)
+
+
+def dot(left, right):
+    return jnp.dot(left, right, preferred_element_type=jnp.float32)
+
+
+def dot3(high, low, ref, lead):
+    top = ref[(*lead, 0)]
+    return dot(high, top) + (dot(high, ref[(*lead, 1)]) + dot(low, top))
+
+
+def operator_steps(
+    n, scale, bound, q, k, v, c, h, taps, skip, tables, twist, outs, filt, tsum, ssum, scratch
+):
+    chi, clo, shi, slo = tables
+    gd, spec, s1s, s2s, dms, ds = scratch
+    width = q.shape[1]
+    rows = 64
+    rt = lambda b, j: taps[pl.ds(3 * b + j, 1), :]
+
+    def lagged(ref, i):
+        base = pl.multiple_of(i * rows, rows)
+        head = pl.multiple_of(jnp.maximum(base - 16, 0), 16)
+        halo = ref[pl.ds(head, 16), :].astype(jnp.float32)
+        halo = jnp.where(i > 0, halo, 0.0)
+        ext = jnp.concatenate((halo, ref[pl.ds(base, rows), :].astype(jnp.float32)), axis=0)
+        return ext[16:], pltpu.roll(ext, 1, 0)[16:], pltpu.roll(ext, 2, 0)[16:]
+
+    def short(ref, b, i):
+        x0, x1, x2 = lagged(ref, i)
+        return rt(b, 0) * x0 + rt(b, 1) * x1 + rt(b, 2) * x2
+
+    def masked(i):
+        base = pl.multiple_of(i * rows, rows)
+        pos = base + lax.broadcasted_iota(jnp.int32, (rows, width), 0)
+        return jnp.where(pos >= bound, c[pl.ds(base, rows), :].astype(jnp.float32), 0.0)
+
+    ssum[...] = jnp.zeros_like(ssum)
+    tsum[...] = jnp.zeros_like(tsum)
+
+    @pl.loop(0, n // rows)
+    def _(i):
+        at = pl.ds(pl.multiple_of(i * rows, rows), rows)
+        s1 = short(k, 1, i)
+        s2 = short(v, 2, i)
+        gated = s1 * s2
+        dmix = masked(i) * short(q, 0, i)
+        s1s[at, :] = s1
+        s2s[at, :] = s2
+        dms[at, :] = dmix
+        split_to(gd, (0,), at, gated)
+        split_to(gd, (1,), at, dmix)
+        ssum[...] += jnp.sum((dmix * gated).reshape(rows // 8, 8, width), axis=0)
+
+    block = min(256, n)
+
+    @pl.loop(0, n // block)
+    def _(j):
+        at = pl.ds(pl.multiple_of(j * block, block), block)
+        ch, cl, sh, sl = chi[at, :], clo[at, :], shi[at, :], slo[at, :]
+        tr, ti = twist[0, at, :], twist[1, at, :]
+        hr = dot(ch, h[...]) + dot(cl, h[...])
+        hi = -(dot(sh, h[...]) + dot(sl, h[...]))
+        hr, hi = hr * tr - hi * ti, hr * ti + hi * tr
+        gr = dot3(ch, cl, gd, (0,))
+        gi = -dot3(sh, sl, gd, (0,))
+        split_to(spec, (0, 0), at, gr * hr - gi * hi)
+        split_to(spec, (0, 1), at, gr * hi + gi * hr)
+        gr, gi = gr * tr - gi * ti, gr * ti + gi * tr
+        dr = dot3(ch, cl, gd, (1,))
+        di = -dot3(sh, sl, gd, (1,))
+        split_to(spec, (1, 0), at, hr * dr + hi * di)
+        split_to(spec, (1, 1), at, hr * di - hi * dr)
+        split_to(spec, (2, 0), at, gr * dr + gi * di)
+        split_to(spec, (2, 1), at, gr * di - gi * dr)
+
+    @pl.loop(0, n // block)
+    def _(j):
+        at = pl.ds(pl.multiple_of(j * block, block), block)
+        ch, cl, sh, sl = chi[at, :], clo[at, :], shi[at, :], slo[at, :]
+        filt[at, :] = (
+            dot3(ch, cl, spec, (2, 0)) - dot3(sh, sl, spec, (2, 1))
+        ) * (scale / n)
+        ds[0, at, :] = (dot3(ch, cl, spec, (0, 0)) - dot3(sh, sl, spec, (0, 1))) * (1.0 / n)
+        ds[1, at, :] = (dot3(ch, cl, spec, (1, 0)) - dot3(sh, sl, spec, (1, 1))) * (1.0 / n)
+
+    ds[:, pl.ds(n, 8), :] = jnp.zeros((3, 8, width), jnp.float32)
+
+    @pl.loop(0, n // rows)
+    def _(i):
+        at = pl.ds(pl.multiple_of(i * rows, rows), rows)
+        s1, s2, dmix = s1s[at, :], s2s[at, :], dms[at, :]
+        d0 = masked(i) * (ds[0, at, :] + skip[...] * (s1 * s2))
+        dg = ds[1, at, :] + skip[...] * dmix
+        for b, (d, ref) in enumerate(((d0, q), (dg * s2, k), (dg * s1, v))):
+            ds[b, at, :] = d
+            for lag, x in enumerate(lagged(ref, i)):
+                tsum[3 * b + lag] += jnp.sum((d * x).reshape(rows // 8, 8, width), axis=0)
+
+    @pl.loop(0, n // rows)
+    def _(i):
+        base = pl.multiple_of(i * rows, rows)
+        for b in range(3):
+            ext = ds[b, pl.ds(base, rows + 8), :]
+            g = rt(b, 0) * ext + rt(b, 1) * pltpu.roll(ext, rows + 7, 0)
+            g = g + rt(b, 2) * pltpu.roll(ext, rows + 6, 0)
+            outs[b][pl.ds(base, rows), :] = g[:rows].astype(jnp.bfloat16)
+
+
+def operator_kernel(n, scale, bound, q, k, v, c, h, taps, skip, *rest):
+    tables, twist = rest[:4], rest[4]
+    outs, filt, tsum, ssum = rest[5:8], rest[8], rest[9], rest[10]
+    operator_steps(
+        n, scale, bound[0], q, k, v, c, h, taps, skip, tables, twist, outs, filt, tsum, ssum, rest[11:]
+    )
+
+
+def scratch_of(n, width):
+    return [
+        pltpu.VMEM((2, 2, n, width), jnp.bfloat16),
+        pltpu.VMEM((3, 2, 2, n, width), jnp.bfloat16),
+        pltpu.VMEM((n, width), jnp.float32),
+        pltpu.VMEM((n, width), jnp.float32),
+        pltpu.VMEM((n, width), jnp.float32),
+        pltpu.VMEM((3, n + 8, width), jnp.float32),
+    ]
+
+
+def to_owner(value):
+    return lax.all_to_all(value, "seq", split_axis=1, concat_axis=0, tiled=True)
+
+
+def to_rows(value):
+    return lax.all_to_all(value, "seq", split_axis=0, concat_axis=1, tiled=True)
+
+
+def dense_body(query_proj, key_proj, value_proj, cotangent, boundary, short_taps, skip_gain, long_filter):
+    tok, width = query_proj.shape[1:]
+    parts = lax.axis_size("seq")
+    n = tok * parts
+    own = width // parts
+    scale = 1.0 / math.sqrt(lax.axis_size("dp") * n)
+    tables, twist = dense_tables(n)
+    first = lax.axis_index("seq") * own
+    taps = lax.dynamic_slice_in_dim(short_taps.reshape(9, width), first, own, axis=1)
+    skip = lax.dynamic_slice_in_dim(skip_gain[None], first, own, axis=1)
+    cols = [to_owner(x[0]) for x in (query_proj, key_proj, value_proj, cotangent)]
+    vmem = pl.BlockSpec(memory_space=pltpu.VMEM)
+    f32, bf16 = jnp.float32, jnp.bfloat16
+    gq, gk, gv, filt, tsum, ssum = pl.pallas_call(
+        functools.partial(operator_kernel, n, scale),
+        out_shape=[jax.ShapeDtypeStruct((n, own), bf16)] * 3
+        + [
+            jax.ShapeDtypeStruct((n, own), f32),
+            jax.ShapeDtypeStruct((9, 8, own), f32),
+            jax.ShapeDtypeStruct((8, own), f32),
+        ],
+        in_specs=[pl.BlockSpec(memory_space=pltpu.SMEM)] + [vmem] * 12,
+        out_specs=[vmem] * 6,
+        scratch_shapes=scratch_of(n, own),
+        compiler_params=pltpu.CompilerParams(vmem_limit_bytes=56 * 2**20),
+    )(boundary, *cols, to_owner(long_filter), taps, skip, *(jnp.asarray(t) for t in tables), jnp.asarray(twist))
+    sums = jnp.concatenate((jnp.sum(tsum, axis=1), jnp.sum(ssum, axis=0, keepdims=True))) * scale
+    pair = [(0, 1), (1, 0)]
+    filt = filt + lax.ppermute(filt, "dp", pair)
+    sums = sums + lax.ppermute(sums, "dp", pair)
+    filter_grad = to_rows(filt.astype(bf16))
+    grads = [to_rows(g)[None] for g in (gq, gk, gv)]
+    return (*grads, filter_grad, sums[:9].reshape(3, 3, own), sums[9])
+
+
 def body(query_proj, key_proj, value_proj, cotangent, boundary, short_taps, skip_gain, long_filter):
     pairs, tok, width = query_proj.shape
     parts = lax.axis_size("seq")
@@ -200,4 +394,9 @@
         P("groups", None, "seq"),
         P(("groups", "seq")),
     )
-    return jax.shard_map(body, mesh=mesh, in_specs=in_specs, out_specs=out_specs, check_vma=False)
+    def chosen(query_proj, *rest):
+        pairs, tok, _ = query_proj.shape
+        dense = pairs == 1 and mesh.shape["dp"] == 2 and tok * mesh.shape["seq"] <= DENSE_LIMIT
+        return (dense_body if dense else body)(query_proj, *rest)
+
+    return jax.shard_map(chosen, mesh=mesh, in_specs=in_specs, out_specs=out_specs, check_vma=False)

time: 413 us -> 205 us (0.50)
  local copies, waits for them, and re-layouts: 96.7 us -> 14.8 us
  matrix products: 63.3 us -> 0 us
  other arithmetic: 35.4 us -> 2.22 us
  Pallas kernels: 0 us -> 31.6 us
  waiting for transfers between devices: 127 us -> 102 us
  blocking collectives: 36.7 us -> 18.4 us
  between operations: 16.3 us -> 1.45 us
    dot_general x21 -> x0, matrix products: 63.3 us -> none  [the longest x12 35.8 us: dot_high(): jnp.dot(left, right, precision=lax.Precision.HIGHEST, preferred_element_t...]
    unnamed x2 -> x0, waiting for transfers between devices: 62.5 us -> none
    all_to_all x6 -> x8, waiting for transfers between devices: 62.7 us -> 101 us  [the longest x5 66.6 us: to_owner(): return lax.all_to_all(value, 'seq', split_axis=1, concat_axis=0, tiled=True)]
    pallas_call x0 -> x1, Pallas kernels: none -> 31.6 us  [dense_body(): pl.pallas_call(functools.partial(operator_kernel, n, scale), out_shape=[j...]
    unnamed x1 -> x0, blocking collectives: 30.3 us -> none
    slice x14 -> x1, local copies, waits for them, and re-layouts: 24.8 us -> 0.57 us  [dense_body(): return (*grads, filter_grad, sums[:9].reshape(3, 3, own), sums[9])]
    reshape x6 -> x2, local copies, waits for them, and re-layouts: 23.5 us -> 0.65 us  [the longest x1 0.61 us: dense_body(): return (*grads, filter_grad, sums[:9].reshape(3, 3, own), sums[9])]
    sub x4 -> x0, other arithmetic: 20.3 us -> none  [the longest x1 8.29 us: correlate_cols(): filt_re * grad_im - filt_im * grad_re]
  transfers between devices with their start and end apart: 9 -> 10, of which waited for: 7 -> 9; matrix products, arithmetic and copies ran while one was open for 13% -> 6% of each run, Pallas kernels for 0% -> 0%
where the time goes in v1:
time: 205 us; the launch traced here: 204 us
  waiting for transfers between devices  102 us (50%)
  starting transfers between devices  33 us (16%)
  Pallas kernels  31.6 us (15%)
  blocking collectives  18.4 us (9%)
  local copies, waits for them, and re-layouts  14.8 us (7%)
  other arithmetic  2.22 us (1%)
    all_to_all x5, waiting for transfers between devices, to_owner(): return lax.all_to_all(value, 'seq', split_axis=1, concat_axis=0, tiled=True)  66.6 us
    all_to_all x3, waiting for transfers between devices, to_rows(): return lax.all_to_all(value, 'seq', split_axis=0, concat_axis=1, tiled=True)  34.5 us
    pallas_call x1, Pallas kernels, dense_body(): pl.pallas_call(functools.partial(operator_kernel, n, scale), out_shape=[j...  31.6 us
    all_to_all x5, starting transfers between devices, to_owner(): return lax.all_to_all(value, 'seq', split_axis=1, concat_axis=0, tiled=True)  21.9 us
    all_to_all x1, blocking collectives, to_rows(): return lax.all_to_all(value, 'seq', split_axis=0, concat_axis=1, tiled=True)  18.4 us
    all_to_all x3, starting transfers between devices, to_rows(): return lax.all_to_all(value, 'seq', split_axis=0, concat_axis=1, tiled=True)  10.9 us
    all_to_all x5, local copies, waits for them, and re-layouts, to_owner(): return lax.all_to_all(value, 'seq', split_axis=1, concat_axis=0, tiled=True)  4.41 us
  transfers between devices with their start and end apart: 10, of which 9 were waited for; matrix products, arithmetic and copies ran while one was open for 6% of the time, Pallas kernels for 0%

profile of v1, /device:TPU:0, one launch (start us, length us, event | category | flops | bytes accessed | tf_op | source)
XLA Modules:
  0.0 203.7 jit_solution(7964083501463832066)
XLA Ops:
  0.6 0.0 copy-start.6
  0.6 1.2 copy.30
  1.9 0.9 copy.19
  2.8 7.4 %all-to-all-start = ((bf16[128,8,256]{2,0,1:T(8,128)(2,1)}), bf16[128,8,256]{2,0,1:T(8,128)(2,1)S(1)}, u32[]{:S(2)}, u32[]{:S(2)}) async-start(bf16[128,8,256]{2,0,1:T(8,128)(2,1)} %copy.19), calls=%async_computation | async-start | bytes 1048576 | tf_op jit(solution)/shard_map/all_to_all | solution.py:263
  10.1 0.0 copy-done.6
  10.1 0.1 copy.31
  10.3 0.9 copy.20
  11.2 0.0 copy-start.8
  11.2 13.5 %all-to-all-done = bf16[128,8,256]{2,0,1:T(8,128)(2,1)S(1)} async-done(((bf16[128,8,256]{2,0,1:T(8,128)(2,1)}), bf16[128,8,256]{2,0,1:T(8,128)(2,1)S(1)}, u32[]{:S(2)}, u32[]{:S(2)}) %all-to-all-start) | async-done | bytes 524320 | tf_op jit(solution)/shard_map/all_to_all | solution.py:263
  24.6 0.0 copy-start
  24.6 3.6 %all-to-all-start.1 = ((bf16[128,8,256]{2,0,1:T(8,128)(2,1)}), bf16[128,8,256]{2,0,1:T(8,128)(2,1)S(1)}, u32[]{:S(2)}, u32[]{:S(2)}) async-start(bf16[128,8,256]{2,0,1:T(8,128)(2,1)} %copy.20), calls=%async_computation.1 | async-start | bytes 1048576 | tf_op jit(solution)/shard_map/all_to_all | solution.py:263
  28.3 0.0 copy-done.7
  28.3 0.1 copy.32
  28.4 0.9 copy.21
  29.3 0.0 copy-start.9
  29.3 13.6 %all-to-all-done.1 = bf16[128,8,256]{2,0,1:T(8,128)(2,1)S(1)} async-done(((bf16[128,8,256]{2,0,1:T(8,128)(2,1)}), bf16[128,8,256]{2,0,1:T(8,128)(2,1)S(1)}, u32[]{:S(2)}, u32[]{:S(2)}) %all-to-all-start.1) | async-done | bytes 524320 | tf_op jit(solution)/shard_map/all_to_all | solution.py:263
  42.9 0.0 copy-start.1
  42.9 0.0 copy-done
  42.9 3.6 %all-to-all-start.2 = ((bf16[128,8,256]{2,0,1:T(8,128)(2,1)}), bf16[128,8,256]{2,0,1:T(8,128)(2,1)S(1)}, u32[]{:S(2)}, u32[]{:S(2)}) async-start(bf16[128,8,256]{2,0,1:T(8,128)(2,1)} %copy.21), calls=%async_computation.2 | async-start | bytes 1048576 | tf_op jit(solution)/shard_map/all_to_all | solution.py:263
  46.6 0.0 copy-done.8
  46.6 0.1 copy.33
  46.7 0.0 copy-start.10
  46.7 0.9 copy.22
  47.6 13.6 %all-to-all-done.2 = bf16[128,8,256]{2,0,1:T(8,128)(2,1)S(1)} async-done(((bf16[128,8,256]{2,0,1:T(8,128)(2,1)}), bf16[128,8,256]{2,0,1:T(8,128)(2,1)S(1)}, u32[]{:S(2)}, u32[]{:S(2)}) %all-to-all-start.2) | async-done | bytes 524320 | tf_op jit(solution)/shard_map/all_to_all | solution.py:263
  61.2 0.0 copy-start.2
  61.2 0.0 copy-done.1
  61.2 3.6 %all-to-all-start.3 = ((bf16[128,8,256]{2,0,1:T(8,128)(2,1)}), bf16[128,8,256]{2,0,1:T(8,128)(2,1)S(1)}, u32[]{:S(2)}, u32[]{:S(2)}) async-start(bf16[128,8,256]{2,0,1:T(8,128)(2,1)} %copy.22), calls=%async_computation.3 | async-start | bytes 1048576 | tf_op jit(solution)/shard_map/all_to_all | solution.py:263
  64.9 0.0 copy-done.9
  64.9 0.8 copy.35
  65.7 13.8 %all-to-all-done.3 = bf16[128,8,256]{2,0,1:T(8,128)(2,1)S(1)} async-done(((bf16[128,8,256]{2,0,1:T(8,128)(2,1)}), bf16[128,8,256]{2,0,1:T(8,128)(2,1)S(1)}, u32[]{:S(2)}, u32[]{:S(2)}) %all-to-all-start.3) | async-done | bytes 524320 | tf_op jit(solution)/shard_map/all_to_all | solution.py:263
  79.6 3.6 %all-to-all-start.4 = ((bf16[128,8,256]{2,0,1:T(8,128)(2,1)}), bf16[128,8,256]{2,0,1:T(8,128)(2,1)S(1)}, u32[]{:S(2)}, u32[]{:S(2)}) async-start(bf16[128,8,256]{2,0,1:T(8,128)(2,1)} %bitcast.43), calls=%async_computation.4 | async-start | bytes 1048576 | tf_op jit(solution)/shard_map/all_to_all | solution.py:263
  83.8 0.0 copy-done.10
  83.9 1.3 dynamic-slice.3
  85.2 0.6 constant_dynamic-slice_fusion.taps
  85.8 12.0 %all-to-all-done.4 = bf16[128,8,256]{2,0,1:T(8,128)(2,1)S(1)} async-done(((bf16[128,8,256]{2,0,1:T(8,128)(2,1)}), bf16[128,8,256]{2,0,1:T(8,128)(2,1)S(1)}, u32[]{:S(2)}, u32[]{:S(2)}) %all-to-all-start.4) | async-done | bytes 524320 | tf_op jit(solution)/shard_map/all_to_all | solution.py:263
  97.9 0.0 copy-done.2
  97.9 0.0 copy-done.3
  97.9 0.8 copy-done.4
  98.7 31.6 %shard_map.172 = (bf16[1024,256]{1,0:T(8,128)(2,1)}, bf16[1024,256]{1,0:T(8,128)(2,1)}, bf16[1024,256]{1,0:T(8,128)(2,1)}, f32[1024,256]{1,0:T(8,128)}, f32[9,8,256]{2,1,0:T(8,128)}, /*index=5*/f32[8,256]{1,0:T(8,128)}) custom-call(s32[1]{0:T(128)S(6)} %copy.36.bound, bf16[1024,256]{1,0:T(8,128)(2,1)} %bitcast.45, bf16[1024,256]{1,0:T(8,128)(2,1)} %bitcast.46, ...), custom_call_target="tpu_custom_call" | custom-call | tf_op jit(solution)/shard_map/pallas_call | solution.py:283
  130.2 18.4 %all_to_all.162 = bf16[8,128,256]{2,1,0:T(8,128)(2,1)S(1)} all-to-all(bf16[8,128,256]{2,1,0:T(8,128)(2,1)} %bitcast.64), channel_id=1, replica_groups=mesh['groups'=2,'dp'=2,'seq'=8] {'seq'}, dimensions={0} | all-to-all | bytes 1048576 | tf_op jit(solution)/shard_map/all_to_all | solution.py:267
  148.7 3.6 %all-to-all-start.5 = ((bf16[8,128,256]{2,1,0:T(8,128)(2,1)}), bf16[8,128,256]{2,1,0:T(8,128)(2,1)S(1)}, u32[]{:S(2)}, u32[]{:S(2)}) async-start(bf16[8,128,256]{2,1,0:T(8,128)(2,1)} %bitcast.63), calls=%async_computation.5 | async-start | bytes 1048576 | tf_op jit(solution)/shard_map/all_to_all | solution.py:267
  152.3 0.0 copy-done.5
  152.3 0.1 collective-permute-start
  152.4 14.1 %all-to-all-done.5 = bf16[8,128,256]{2,1,0:T(8,128)(2,1)S(1)} async-done(((bf16[8,128,256]{2,1,0:T(8,128)(2,1)}), bf16[8,128,256]{2,1,0:T(8,128)(2,1)S(1)}, u32[]{:S(2)}, u32[]{:S(2)}) %all-to-all-start.5) | async-done | bytes 524320 | tf_op jit(solution)/shard_map/all_to_all | solution.py:267
  166.5 3.6 %all-to-all-start.7 = ((bf16[8,128,256]{2,1,0:T(8,128)(2,1)}), bf16[8,128,256]{2,1,0:T(8,128)(2,1)S(1)}, u32[]{:S(2)}, u32[]{:S(2)}) async-start(bf16[8,128,256]{2,1,0:T(8,128)(2,1)} %bitcast.15), calls=%async_computation.7 | async-start | bytes 1048576 | tf_op jit(solution)/shard_map/all_to_all | solution.py:267
  170.1 0.0 copy-start.11
  170.2 0.0 collective-permute-done
  170.2 2.2 %add_convert_fusion = bf16[1024,256]{1,0:T(8,128)(2,1)} fusion(f32[1024,256]{1,0:T(8,128)S(1)} %copy-done.5, f32[1024,256]{1,0:T(8,128)} %collective-permute-done), kind=kLoop, calls=%fused_computation | loop fusion | flops 524288 | bytes 2621440 | tf_op jit(solution)/shard_map/convert_element_type | solution.py:300
  172.3 12.3 %all-to-all-done.7 = bf16[8,128,256]{2,1,0:T(8,128)(2,1)S(1)} async-done(((bf16[8,128,256]{2,1,0:T(8,128)(2,1)}), bf16[8,128,256]{2,1,0:T(8,128)(2,1)S(1)}, u32[]{:S(2)}, u32[]{:S(2)}) %all-to-all-start.7) | async-done | bytes 524320 | tf_op jit(solution)/shard_map/all_to_all | solution.py:267
  184.6 3.6 %all-to-all-start.8 = ((bf16[8,128,256]{2,1,0:T(8,128)(2,1)}), bf16[8,128,256]{2,1,0:T(8,128)(2,1)S(1)}, u32[]{:S(2)}, u32[]{:S(2)}) async-start(bf16[8,128,256]{2,1,0:T(8,128)(2,1)} %bitcast.17), calls=%async_computation.8 | async-start | bytes 1048576 | tf_op jit(solution)/shard_map/all_to_all | solution.py:267
  188.2 0.0 copy-done.12
  188.2 0.0 copy-done.11
  188.3 0.1 collective-permute-start.1
  188.4 1.2 collective-permute-done.1
  189.5 0.6 slice.9
  190.1 0.6 reshape.54
  190.7 0.3 copy.25
  191.0 1.0 broadcast_in_dim.14
  192.1 0.3 copy.24
  192.3 1.0 broadcast_in_dim.13
  193.4 0.3 copy.26
  193.7 1.0 broadcast_in_dim.15
  194.7 8.2 %all-to-all-done.8 = bf16[8,128,256]{2,1,0:T(8,128)(2,1)S(1)} async-done(((bf16[8,128,256]{2,1,0:T(8,128)(2,1)}), bf16[8,128,256]{2,1,0:T(8,128)(2,1)S(1)}, u32[]{:S(2)}, u32[]{:S(2)}) %all-to-all-start.8) | async-done | bytes 524320 | tf_op jit(solution)/shard_map/all_to_all | solution.py:267
  202.9 0.8 copy.29
  (10 shorter events, 0.1 us)
Async XLA Ops:
  0.6 9.5 %copy-start.6 = (bf16[1,128,2048]{2,1,0:T(8,128)(2,1)S(1)}, bf16[1,128,2048]{2,1,0:T(8,128)(2,1)}, u32[]{:S(2)}) copy-start(bf16[1,128,2048]{2,1,0:T(8,128)(2,1)} %param.14) | copy-start | bytes 1572868
  2.8 25.5 %copy-start.7 = (bf16[1,128,2048]{2,1,0:T(8,128)(2,1)S(1)}, bf16[1,128,2048]{2,1,0:T(8,128)(2,1)}, u32[]{:S(2)}) copy-start(bf16[1,128,2048]{2,1,0:T(8,128)(2,1)} %param.15) | copy-start | bytes 1572868
  2.8 21.9 %all-to-all-start = ((bf16[128,8,256]{2,0,1:T(8,128)(2,1)}), bf16[128,8,256]{2,0,1:T(8,128)(2,1)S(1)}, u32[]{:S(2)}, u32[]{:S(2)}) async-start(bf16[128,8,256]{2,0,1:T(8,128)(2,1)} %copy.19), calls=%async_computation | async-start | bytes 1048576 | tf_op jit(solution)/shard_map/all_to_all | solution.py:263
  11.2 35.4 %copy-start.8 = (bf16[1,128,2048]{2,1,0:T(8,128)(2,1)S(1)}, bf16[1,128,2048]{2,1,0:T(8,128)(2,1)}, u32[]{:S(2)}) copy-start(bf16[1,128,2048]{2,1,0:T(8,128)(2,1)} %param.16) | copy-start | bytes 1572868
  24.6 18.3 %copy-start = (bf16[128,8,256]{2,0,1:T(8,128)(2,1)}, bf16[128,8,256]{2,0,1:T(8,128)(2,1)S(1)}, u32[]{:S(2)}) copy-start(bf16[128,8,256]{2,0,1:T(8,128)(2,1)S(1)} %all-to-all-done) | copy-start | bytes 1572868
  24.6 18.3 %all-to-all-start.1 = ((bf16[128,8,256]{2,0,1:T(8,128)(2,1)}), bf16[128,8,256]{2,0,1:T(8,128)(2,1)S(1)}, u32[]{:S(2)}, u32[]{:S(2)}) async-start(bf16[128,8,256]{2,0,1:T(8,128)(2,1)} %copy.20), calls=%async_computation.1 | async-start | bytes 1048576 | tf_op jit(solution)/shard_map/all_to_all | solution.py:263
  29.3 35.6 %copy-start.9 = (bf16[128,2048]{1,0:T(8,128)(2,1)S(1)}, bf16[128,2048]{1,0:T(8,128)(2,1)}, u32[]{:S(2)}) copy-start(bf16[128,2048]{1,0:T(8,128)(2,1)} %param.20) | copy-start | bytes 1572868
  42.9 18.3 %copy-start.1 = (bf16[128,8,256]{2,0,1:T(8,128)(2,1)}, bf16[128,8,256]{2,0,1:T(8,128)(2,1)S(1)}, u32[]{:S(2)}) copy-start(bf16[128,8,256]{2,0,1:T(8,128)(2,1)S(1)} %all-to-all-done.1) | copy-start | bytes 1572868
  42.9 18.3 %all-to-all-start.2 = ((bf16[128,8,256]{2,0,1:T(8,128)(2,1)}), bf16[128,8,256]{2,0,1:T(8,128)(2,1)S(1)}, u32[]{:S(2)}, u32[]{:S(2)}) async-start(bf16[128,8,256]{2,0,1:T(8,128)(2,1)} %copy.21), calls=%async_computation.2 | async-start | bytes 1048576 | tf_op jit(solution)/shard_map/all_to_all | solution.py:263
  46.7 37.1 %copy-start.10 = (f32[3,3,2048]{2,1,0:T(4,128)S(1)}, f32[3,3,2048]{2,1,0:T(4,128)}, u32[]{:S(2)}) copy-start(f32[3,3,2048]{2,1,0:T(4,128)} %param.18) | copy-start | bytes 221188
  61.2 36.6 %copy-start.2 = (bf16[128,8,256]{2,0,1:T(8,128)(2,1)}, bf16[128,8,256]{2,0,1:T(8,128)(2,1)S(1)}, u32[]{:S(2)}) copy-start(bf16[128,8,256]{2,0,1:T(8,128)(2,1)S(1)} %all-to-all-done.2) | copy-start | bytes 1572868
  61.2 18.3 %all-to-all-start.3 = ((bf16[128,8,256]{2,0,1:T(8,128)(2,1)}), bf16[128,8,256]{2,0,1:T(8,128)(2,1)S(1)}, u32[]{:S(2)}, u32[]{:S(2)}) async-start(bf16[128,8,256]{2,0,1:T(8,128)(2,1)} %copy.22), calls=%async_computation.3 | async-start | bytes 1048576 | tf_op jit(solution)/shard_map/all_to_all | solution.py:263
  79.6 18.3 %copy-start.3 = (bf16[128,8,256]{2,0,1:T(8,128)(2,1)}, bf16[128,8,256]{2,0,1:T(8,128)(2,1)S(1)}, u32[]{:S(2)}) copy-start(bf16[128,8,256]{2,0,1:T(8,128)(2,1)S(1)} %all-to-all-done.3) | copy-start | bytes 1572868
  79.6 18.3 %all-to-all-start.4 = ((bf16[128,8,256]{2,0,1:T(8,128)(2,1)}), bf16[128,8,256]{2,0,1:T(8,128)(2,1)S(1)}, u32[]{:S(2)}, u32[]{:S(2)}) async-start(bf16[128,8,256]{2,0,1:T(8,128)(2,1)} %bitcast.43), calls=%async_computation.4 | async-start | bytes 1048576 | tf_op jit(solution)/shard_map/all_to_all | solution.py:263
  97.9 0.8 copy-start.4
  130.2 22.1 %copy-start.5 = (f32[1024,256]{1,0:T(8,128)S(1)}, f32[1024,256]{1,0:T(8,128)}, u32[]{:S(2)}) copy-start(f32[1024,256]{1,0:T(8,128)} %get-tuple-element.15) | copy-start | bytes 3145732
  148.7 17.8 %all-to-all-start.5 = ((bf16[8,128,256]{2,1,0:T(8,128)(2,1)}), bf16[8,128,256]{2,1,0:T(8,128)(2,1)S(1)}, u32[]{:S(2)}, u32[]{:S(2)}) async-start(bf16[8,128,256]{2,1,0:T(8,128)(2,1)} %bitcast.63), calls=%async_computation.5 | async-start | bytes 1048576 | tf_op jit(solution)/shard_map/all_to_all | solution.py:267
  152.3 17.8 %collective-permute-start = (f32[1024,256]{1,0:T(8,128)S(1)}, f32[1024,256]{1,0:T(8,128)}, u32[]{:S(2)}, u32[]{:S(2)}) collective-permute-start(f32[1024,256]{1,0:T(8,128)S(1)} %copy-done.5), channel_id=1, source_target_pairs={{0,8},{8,0},{1,9},{9,1},{2,10},{10,2},{3,11},{11,3},{4,12},{12,4},... | collective-permute-start | bytes 3145736 | tf_op jit(solution)/shard_map/ppermute | solution.py:298
  166.5 18.1 %all-to-all-start.7 = ((bf16[8,128,256]{2,1,0:T(8,128)(2,1)}), bf16[8,128,256]{2,1,0:T(8,128)(2,1)S(1)}, u32[]{:S(2)}, u32[]{:S(2)}) async-start(bf16[8,128,256]{2,1,0:T(8,128)(2,1)} %bitcast.15), calls=%async_computation.7 | async-start | bytes 1048576 | tf_op jit(solution)/shard_map/all_to_all | solution.py:267
  170.1 18.1 %copy-start.12 = (f32[8,256]{1,0:T(8,128)S(1)}, f32[8,256]{1,0:T(8,128)}, u32[]{:S(2)}) copy-start(f32[8,256]{1,0:T(8,128)} %get-tuple-element.17) | copy-start | bytes 24580
  170.1 18.1 %copy-start.11 = (f32[9,8,256]{2,1,0:T(8,128)S(1)}, f32[9,8,256]{2,1,0:T(8,128)}, u32[]{:S(2)}) copy-start(f32[9,8,256]{2,1,0:T(8,128)} %get-tuple-element.16) | copy-start | bytes 221188
  184.6 18.3 %all-to-all-start.8 = ((bf16[8,128,256]{2,1,0:T(8,128)(2,1)}), bf16[8,128,256]{2,1,0:T(8,128)(2,1)S(1)}, u32[]{:S(2)}, u32[]{:S(2)}) async-start(bf16[8,128,256]{2,1,0:T(8,128)(2,1)} %bitcast.17), calls=%async_computation.8 | async-start | bytes 1048576 | tf_op jit(solution)/shard_map/all_to_all | solution.py:267
  188.3 1.2 collective-permute-start.1

commit v2 on v0

--- a/solution.py
+++ b/solution.py
@@ -1,9 +1,17 @@
+import functools
 import math
 
 import jax
 import jax.numpy as jnp
+import numpy as np
 from jax import lax
+from jax.experimental import pallas as pl
+from jax.experimental.pallas import tpu as pltpu
 from jax.sharding import PartitionSpec as P
+
+DENSE_LIMIT = 1024
+LANES = 128
+MESH = pl.DeviceIdType.MESH
 
 
 def passed_along(value, axis, by):
@@ -108,6 +116,361 @@
     return (back, filt_part)
 
 
+def phase_tables(n):
+    index = 4 * np.arange(n, dtype=np.int64) + 1
+    unit = 2.0 * np.pi / (16 * n)
+    fine = (index[:, None] * index[None, :LANES] % (16 * n)) * unit
+    coarse = (index[:, None] * (4 * LANES * np.arange(n // LANES))[None, :] % (16 * n)) * unit
+    turn = index[:, None] * unit
+    pack = lambda x: np.stack((np.cos(x), np.sin(x))).astype(np.float32)
+    return pack(fine), pack(np.concatenate((coarse, turn), axis=1))
+
+
+def split_to(ref, lead, rows, value, cols=slice(None)):
+    high = value.astype(jnp.bfloat16)
+    ref[(*lead, 0, rows, cols)] = high
+    ref[(*lead, 1, rows, cols)] = (value - high.astype(jnp.float32)).astype(jnp.bfloat16)
+
+
+def dot(left, right):
+    return jnp.dot(left, right, preferred_element_type=jnp.float32)
+
+
+def dot3(high, low, ref, lead):
+    top = ref[(*lead, 0)]
+    return dot(high, top) + (dot(high, ref[(*lead, 1)]) + dot(low, top))
+
+
+def operator_kernel(
+    n, parts, scale, bound, q_in, k_in, v_in, c_in, h_in, taps_in, skip_in, fine, coarse,
+    gq_out, gk_out, gv_out, f_out, taps_out, skip_out,
+    bufs, cosines, sines, gd, spec, hspec, gspec, s1s, s2s, dms, ds, filt, fother, fown, stage,
+    taps, sums, sother, tsum, send_sem, recv_sem, local_sem, dp_send, dp_recv,
+):
+    tok = n // parts
+    width = bufs.shape[2]
+    half = width // 2
+    rows = 64
+    block = min(256, n)
+    me = lax.axis_index("seq")
+    core = lax.axis_index("dp")
+    partner = {"dp": 1 - core}
+    f32, bf16 = jnp.float32, jnp.bfloat16
+    mine = pl.ds(pl.multiple_of(me * tok, tok), tok)
+    my_half = pl.ds(pl.multiple_of(core * half, half), half)
+    other_half = pl.ds(pl.multiple_of((1 - core) * half, half), half)
+
+    def cols_of(owner):
+        return pl.ds(pl.multiple_of(owner * width, width), width)
+
+    def half_cols_of(owner):
+        return pl.ds(pl.multiple_of(owner * width + core * half, half), half)
+
+    peers = [lax.rem(me + s, parts) for s in range(parts)]
+
+    barrier = pltpu.get_barrier_semaphore()
+    for s in range(1, parts):
+        pl.semaphore_signal(barrier, inc=1, device_id={"seq": peers[s]}, device_id_type=MESH)
+    pl.semaphore_signal(barrier, inc=1, device_id=partner, device_id_type=MESH)
+    pl.semaphore_wait(barrier, parts)
+
+    def exchange(a, source, target):
+        own = pltpu.make_async_copy(source(me), target, local_sem.at[a])
+        own.start()
+        copies = []
+        for s in range(1, parts):
+            copy = pltpu.make_async_remote_copy(
+                src_ref=source(peers[s]),
+                dst_ref=target,
+                send_sem=send_sem.at[a, s],
+                recv_sem=recv_sem.at[a, s],
+                device_id={"seq": peers[s]},
+                device_id_type=MESH,
+            )
+            copy.start()
+            copies.append(copy)
+        return own, copies
+
+    def arrived(moved):
+        moved[0].wait()
+        for copy in moved[1]:
+            copy.wait_recv()
+
+    def to_partner(i, source, target):
+        return pltpu.make_async_remote_copy(
+            src_ref=source,
+            dst_ref=target,
+            send_sem=dp_send.at[i],
+            recv_sem=dp_recv.at[i],
+            device_id=partner,
+            device_id_type=MESH,
+        )
+
+    hb, kb, vb, qb, cb = (bufs.at[i] for i in range(5))
+    h_moved = exchange(0, lambda o: h_in.at[:, half_cols_of(o)], hb.at[mine, my_half])
+    ins = [
+        exchange(1 + i, lambda o, x=x: x.at[0, :, cols_of(o)], bufs.at[1 + i, mine, :])
+        for i, x in enumerate((k_in, v_in, q_in, c_in))
+    ]
+
+    own_cols = cols_of(me)
+    taps[pl.ds(0, 9), :] = taps_in[:, own_cols]
+    taps[pl.ds(9, 1), :] = skip_in[:, own_cols]
+    tsum[...] = jnp.zeros_like(tsum)
+    ds[:, pl.ds(n, 8), :] = jnp.zeros((3, 8, width), f32)
+
+    @pl.loop(0, n // rows)
+    def _(i):
+        at = pl.ds(pl.multiple_of(i * rows, rows), rows)
+        fr, fi = fine[0, at, :], fine[1, at, :]
+        cr, ci = coarse[0, at, :], coarse[1, at, :]
+        for a in range(n // LANES):
+            ar, ai = cr[:, a : a + 1], ci[:, a : a + 1]
+            cols = slice(a * LANES, (a + 1) * LANES)
+            split_to(cosines, (), at, fr * ar - fi * ai, cols)
+            split_to(sines, (), at, fr * ai + fi * ar, cols)
+
+    def tap(b, j):
+        return taps[pl.ds(3 * b + j, 1), :]
+
+    def gain():
+        return taps[pl.ds(9, 1), :]
+
+    def at_rows(i):
+        return pl.ds(pl.multiple_of(i * rows, rows), rows)
+
+    def lagged(ref, i):
+        head = pl.multiple_of(jnp.maximum(i * rows - 16, 0), 16)
+        halo = jnp.where(i > 0, ref[pl.ds(head, 16), :].astype(f32), 0.0)
+        ext = jnp.concatenate((halo, ref[at_rows(i), :].astype(f32)), axis=0)
+        return ext[16:], pltpu.roll(ext, 1, 0)[16:], pltpu.roll(ext, 2, 0)[16:]
+
+    def short(b, lags):
+        return tap(b, 0) * lags[0] + tap(b, 1) * lags[1] + tap(b, 2) * lags[2]
+
+    def add_sum(i, value):
+        tsum[i] += jnp.sum(value.reshape(rows // 8, 8, width), axis=0)
+
+    def add_taps(b, d, lags):
+        for j in range(3):
+            add_sum(3 * b + j, d * lags[j])
+
+    def short_back(b):
+        @pl.loop(0, n // rows)
+        def _(i):
+            ext = ds[b, pl.ds(pl.multiple_of(i * rows, rows), rows + 8), :]
+            g = tap(b, 0) * ext + tap(b, 1) * pltpu.roll(ext, rows + 7, 0)
+            g = g + tap(b, 2) * pltpu.roll(ext, rows + 6, 0)
+            stage[b, at_rows(i), :] = g[:rows].astype(bf16)
+
+    def blocks(table, at):
+        return table[0, at, :], table[1, at, :]
+
+    def inverse(b, at):
+        ch, cl = blocks(cosines, at)
+        sh, sl = blocks(sines, at)
+        return dot3(ch, cl, spec, (b, 0)) - dot3(sh, sl, spec, (b, 1))
+
+    def turned(at, re, im):
+        last = coarse.shape[2] - 1
+        tr, ti = coarse[0, at, last:], coarse[1, at, last:]
+        return re * tr - im * ti, re * ti + im * tr
+
+    def at_block(j):
+        return pl.ds(pl.multiple_of(j * block, block), block)
+
+    arrived(h_moved)
+    h_relay = to_partner(0, hb.at[:, my_half], hb.at[:, my_half])
+    h_relay.start()
+    arrived(ins[0])
+    arrived(ins[1])
+
+    @pl.loop(0, n // rows)
+    def _(i):
+        at = at_rows(i)
+        s1 = short(1, lagged(kb, i))
+        s2 = short(2, lagged(vb, i))
+        s1s[at, :] = s1
+        s2s[at, :] = s2
+        split_to(gd, (0,), at, s1 * s2)
+
+    h_relay.wait_recv()
+
+    @pl.loop(0, n // block)
+    def _(j):
+        at = at_block(j)
+        ch, cl = blocks(cosines, at)
+        sh, sl = blocks(sines, at)
+        h = hb[...]
+        hr, hi = turned(at, dot(ch, h) + dot(cl, h), -(dot(sh, h) + dot(sl, h)))
+        hspec[0, at, :], hspec[1, at, :] = hr, hi
+        gr, gi = dot3(ch, cl, gd, (0,)), -dot3(sh, sl, gd, (0,))
+        split_to(spec, (0, 0), at, gr * hr - gi * hi)
+        split_to(spec, (0, 1), at, gr * hi + gi * hr)
+        gspec[0, at, :], gspec[1, at, :] = turned(at, gr, gi)
+
+    @pl.loop(0, n // block)
+    def _(j):
+        at = at_block(j)
+        ds[0, at, :] = inverse(0, at) * (1.0 / n)
+
+    arrived(ins[2])
+    arrived(ins[3])
+
+    @pl.loop(0, n // rows)
+    def _(i):
+        at = at_rows(i)
+        pos = i * rows + lax.broadcasted_iota(jnp.int32, (rows, width), 0)
+        dout = jnp.where(pos >= bound[0], cb[at, :].astype(f32), 0.0)
+        gated = s1s[at, :] * s2s[at, :]
+        lags = lagged(qb, i)
+        dmix = dout * short(0, lags)
+        d = dout * (ds[0, at, :] + gain() * gated)
+        ds[0, at, :] = d
+        dms[at, :] = dmix
+        split_to(gd, (1,), at, dmix)
+        add_sum(9, dmix * gated)
+        add_taps(0, d, lags)
+
+    def send_back(b, out):
+        short_back(b)
+        return exchange(5 + b, lambda o: stage.at[b, rows_of(o), :], out.at[0, :, own_cols])
+
+    def rows_of(owner):
+        return pl.ds(pl.multiple_of(owner * tok, tok), tok)
+
+    gq_moved = send_back(0, gq_out)
+
+    @pl.loop(0, n // block)
+    def _(j):
+        at = at_block(j)
+        ch, cl = blocks(cosines, at)
+        sh, sl = blocks(sines, at)
+        dr, di = dot3(ch, cl, gd, (1,)), -dot3(sh, sl, gd, (1,))
+        hr, hi = hspec[0, at, :], hspec[1, at, :]
+        split_to(spec, (1, 0), at, hr * dr + hi * di)
+        split_to(spec, (1, 1), at, hr * di - hi * dr)
+        gr, gi = gspec[0, at, :], gspec[1, at, :]
+        split_to(spec, (2, 0), at, gr * dr + gi * di)
+        split_to(spec, (2, 1), at, gr * di - gi * dr)
+
+    @pl.loop(0, n // block)
+    def _(j):
+        at = at_block(j)
+        ds[1, at, :] = inverse(1, at) * (1.0 / n)
+
+    @pl.loop(0, n // rows)
+    def _(i):
+        at = at_rows(i)
+        dg = ds[1, at, :] + gain() * dms[at, :]
+        for b, other, ref in ((1, s2s, kb), (2, s1s, vb)):
+            d = dg * other[at, :]
+            ds[b, at, :] = d
+            add_taps(b, d, lagged(ref, i))
+
+    gk_moved = send_back(1, gk_out)
+    gv_moved = send_back(2, gv_out)
+
+    @pl.loop(0, n // block)
+    def _(j):
+        at = at_block(j)
+        filt[at, :] = inverse(2, at) * (scale / n)
+
+    f_add = to_partner(1, filt.at[:, other_half], fother)
+    f_add.start()
+    sums[...] = jnp.zeros_like(sums)
+    sums[pl.ds(0, 10), :] = jnp.sum(tsum[...], axis=1) * scale
+    s_add = to_partner(2, sums, sother)
+    s_add.start()
+    f_add.wait_recv()
+
+    @pl.loop(0, n // rows)
+    def _(i):
+        at = at_rows(i)
+        fown[at, :] = (filt[at, my_half] + fother[at, :]).astype(bf16)
+
+    f_moved = exchange(8, lambda o: fown.at[rows_of(o), :], f_out.at[:, half_cols_of(me)])
+    own_relay = to_partner(3, fown.at[mine, :], f_out.at[:, half_cols_of(me)])
+    own_relay.start()
+    s_add.wait_recv()
+    total = sums[...] + sother[...]
+    for b in range(3):
+        taps_out[b] = total[3 * b : 3 * b + 3]
+    skip_out[...] = total[9:10]
+
+    relays = [own_relay]
+    for s in range(1, parts):
+        f_moved[1][s - 1].wait_recv()
+        block_cols = half_cols_of(lax.rem(me + parts - s, parts))
+        relay = to_partner(3 + s, f_out.at[:, block_cols], f_out.at[:, block_cols])
+        relay.start()
+        relays.append(relay)
+    f_moved[0].wait()
+    for moved in (gq_moved, gk_moved, gv_moved):
+        arrived(moved)
+    for relay in relays:
+        relay.wait_recv()
+    for moved in (h_moved, *ins, gq_moved, gk_moved, gv_moved, f_moved):
+        for copy in moved[1]:
+            copy.wait_send()
+    for copy in (h_relay, f_add, s_add, *relays):
+        copy.wait_send()
+
+
+def dense_body(query_proj, key_proj, value_proj, cotangent, boundary, short_taps, skip_gain, long_filter):
+    tok, width = query_proj.shape[1:]
+    parts = lax.axis_size("seq")
+    n = tok * parts
+    own = width // parts
+    scale = 1.0 / math.sqrt(lax.axis_size("dp") * n)
+    fine, coarse = phase_tables(n)
+    vmem = pl.BlockSpec(memory_space=pltpu.VMEM)
+    anywhere = pl.BlockSpec(memory_space=pl.ANY)
+    f32, bf16 = jnp.float32, jnp.bfloat16
+    shape = jax.ShapeDtypeStruct
+    dma = pltpu.SemaphoreType.DMA
+    gq, gk, gv, filter_grad, taps_grad, skip_grad = pl.pallas_call(
+        functools.partial(operator_kernel, n, parts, scale),
+        out_shape=[shape((1, tok, width), bf16)] * 3
+        + [shape((tok, width), bf16), shape((3, 3, own), f32), shape((1, own), f32)],
+        in_specs=[pl.BlockSpec(memory_space=pltpu.SMEM)] + [anywhere] * 5 + [vmem] * 4,
+        out_specs=[anywhere] * 4 + [vmem] * 2,
+        scratch_shapes=[
+            pltpu.VMEM((5, n, own), bf16),
+            pltpu.VMEM((2, n, n), bf16),
+            pltpu.VMEM((2, n, n), bf16),
+            pltpu.VMEM((2, 2, n, own), bf16),
+            pltpu.VMEM((3, 2, 2, n, own), bf16),
+            pltpu.VMEM((2, n, own), f32),
+            pltpu.VMEM((2, n, own), f32),
+            pltpu.VMEM((n, own), f32),
+            pltpu.VMEM((n, own), f32),
+            pltpu.VMEM((n, own), f32),
+            pltpu.VMEM((3, n + 8, own), f32),
+            pltpu.VMEM((n, own), f32),
+            pltpu.VMEM((n, own // 2), f32),
+            pltpu.VMEM((n, own // 2), bf16),
+            pltpu.VMEM((3, n, own), bf16),
+            pltpu.VMEM((16, own), f32),
+            pltpu.VMEM((16, own), f32),
+            pltpu.VMEM((16, own), f32),
+            pltpu.VMEM((10, 8, own), f32),
+            dma((9, parts)),
+            dma((9, parts)),
+            dma((9,)),
+            dma((3 + parts,)),
+            dma((3 + parts,)),
+        ],
+        compiler_params=pltpu.CompilerParams(
+            collective_id=0, has_side_effects=True, vmem_limit_bytes=56 * 2**20
+        ),
+    )(
+        boundary, query_proj, key_proj, value_proj, cotangent, long_filter,
+        short_taps.reshape(9, width), skip_gain[None], jnp.asarray(fine), jnp.asarray(coarse),
+    )
+    return gq, gk, gv, filter_grad, taps_grad, skip_grad.reshape(own)
+
+
 def body(query_proj, key_proj, value_proj, cotangent, boundary, short_taps, skip_gain, long_filter):
     pairs, tok, width = query_proj.shape
     parts = lax.axis_size("seq")
@@ -200,4 +563,9 @@
         P("groups", None, "seq"),
         P(("groups", "seq")),
     )
-    return jax.shard_map(body, mesh=mesh, in_specs=in_specs, out_specs=out_specs, check_vma=False)
+    def chosen(query_proj, *rest):
+        pairs, tok, _ = query_proj.shape
+        dense = pairs == 1 and mesh.shape["dp"] == 2 and tok * mesh.shape["seq"] <= DENSE_LIMIT
+        return (dense_body if dense else body)(query_proj, *rest)
+
+    return jax.shard_map(chosen, mesh=mesh, in_specs=in_specs, out_specs=out_specs, check_vma=False)

time: 413 us -> 114 us (0.28)
  waiting for transfers between devices: 127 us -> 0 us
  Pallas kernels: 0 us -> 102 us
  local copies, waits for them, and re-layouts: 96.7 us -> 8.01 us
  matrix products: 63.3 us -> 0 us
  blocking collectives: 36.7 us -> 0 us
  other arithmetic: 35.4 us -> 0 us
  starting transfers between devices: 32.3 us -> 0 us
  between operations: 16.3 us -> 1.3 us
    pallas_call x0 -> x1, Pallas kernels: none -> 102 us  [dense_body(): pl.pallas_call(functools.partial(operator_kernel, n, parts, scale), out_s...]
    dot_general x21 -> x0, matrix products: 63.3 us -> none  [the longest x12 35.8 us: dot_high(): jnp.dot(left, right, precision=lax.Precision.HIGHEST, preferred_element_t...]
    all_to_all x6 -> x0, waiting for transfers between devices: 62.7 us -> none  [the longest x1 21.2 us: body(): lax.all_to_all(jnp.transpose(gated, (0, 2, 1)), 'seq', split_axis=1, conc...]
    unnamed x2 -> x0, waiting for transfers between devices: 62.5 us -> none
    unnamed x1 -> x0, blocking collectives: 30.3 us -> none
    all_to_all x6 -> x0, starting transfers between devices: 26 us -> none  [the longest x1 4.88 us: body(): lax.all_to_all(jnp.transpose(long_filter), 'seq', split_axis=0, concat_ax...]
    slice x14 -> x0, local copies, waits for them, and re-layouts: 24.8 us -> none  [the longest x3 17.4 us: inverse_half(): wide_im = wide[:, :, 1]]
    reshape x6 -> x1, local copies, waits for them, and re-layouts: 23.5 us -> 1.59 us  [dense_body(): short_taps.reshape(9, width)]
  transfers between devices with their start and end apart: 9 -> 0, of which waited for: 7 -> 0; matrix products, arithmetic and copies ran while one was open for 13% -> 0% of each run, Pallas kernels for 0% -> 0%
where the time goes in v2:
time: 114 us; the launch traced here: 112 us
  Pallas kernels  102 us (89%)
  local copies, waits for them, and re-layouts  8.01 us (7%)
  between operations  1.3 us (1%)
    pallas_call x1, Pallas kernels, dense_body(): pl.pallas_call(functools.partial(operator_kernel, n, parts, scale), out_s...  102 us
    unnamed x16, local copies, waits for them, and re-layouts  6.42 us

profile of v2, /device:TPU:0, one launch (start us, length us, event | category | flops | bytes accessed | tf_op | source)
XLA Modules:
  0.0 111.7 jit_solution(3532733154187213422)
XLA Ops:
  1.3 1.6 %reshape.18.taps_in = f32[9,2048]{1,0:T(8,128)} reshape(f32[3,3,2048]{2,1,0:T(4,128)} %param.15) | data formatting | bytes 147456 | tf_op jit(solution)/shard_map/reshape | solution.py:469
  2.9 102.4 %shard_map.145 = (bf16[1,128,2048]{2,1,0:T(8,128)(2,1)}, bf16[1,128,2048]{2,1,0:T(8,128)(2,1)}, bf16[1,128,2048]{2,1,0:T(8,128)(2,1)}, bf16[128,2048]{1,0:T(8,12...) custom-call(s32[1]{0:T(128)S(6)} %copy.22.bound, bf16[1,128,2048]{2,1,0:T(8,128)(2,1)} %q_in.1, ...), custom_call_target="tpu_custom_call" | custom-call | tf_op jit(solution)/shard_map/pallas_call | solution.py:432
  105.3 0.0 copy-start.2
  105.3 1.9 %copy.23 = bf16[1,128,2048]{2,1,0:T(8,128)(2,1)} copy(bf16[1,128,2048]{2,1,0:T(8,128)(2,1)} %get-tuple-element.24) | data formatting | bytes 1048576
  107.2 0.0 copy-done.2
  107.2 0.0 copy-start.1
  107.2 0.8 copy.24
  108.0 0.4 copy-done.1
  108.5 0.0 copy-start
  108.5 0.8 copy.25
  109.3 0.4 copy-done
  109.7 0.0 copy-start.3
  109.7 0.8 copy.26
  110.5 0.0 copy-done.3
  110.5 0.0 copy-start.4
  110.5 0.6 copy.27
  111.1 0.1 copy-done.4
  111.2 0.6 copy.28
Async XLA Ops:
  105.3 2.0 %copy-start.2 = (bf16[1,128,2048]{2,1,0:T(8,128)(2,1)S(1)}, bf16[1,128,2048]{2,1,0:T(8,128)(2,1)}, u32[]{:S(2)}) copy-start(bf16[1,128,2048]{2,1,0:T(8,128)(2,1)} %get-tuple-element.25) | copy-start | bytes 1572868
  107.2 1.2 %copy-start.1 = (bf16[1,128,2048]{2,1,0:T(8,128)(2,1)S(1)}, bf16[1,128,2048]{2,1,0:T(8,128)(2,1)}, u32[]{:S(2)}) copy-start(bf16[1,128,2048]{2,1,0:T(8,128)(2,1)} %get-tuple-element.26) | copy-start | bytes 1572868
  108.5 1.2 %copy-start = (bf16[128,2048]{1,0:T(8,128)(2,1)S(1)}, bf16[128,2048]{1,0:T(8,128)(2,1)}, u32[]{:S(2)}) copy-start(bf16[128,2048]{1,0:T(8,128)(2,1)} %get-tuple-element.27) | copy-start | bytes 1572868
  109.7 0.8 copy-start.3
  110.5 0.7 copy-start.4

commit v3 on v2

--- a/solution.py
+++ b/solution.py
@@ -214,7 +214,8 @@
     ]
 
     own_cols = cols_of(me)
-    taps[pl.ds(0, 9), :] = taps_in[:, own_cols]
+    for b in range(3):
+        taps[pl.ds(3 * b, 3), :] = taps_in[b, :, own_cols]
     taps[pl.ds(9, 1), :] = skip_in[:, own_cols]
     tsum[...] = jnp.zeros_like(tsum)
     ds[:, pl.ds(n, 8), :] = jnp.zeros((3, 8, width), f32)
@@ -417,6 +418,17 @@
         copy.wait_send()
 
 
+def copy_kernel(*refs):
+    count = len(refs) // 2
+    copies = [
+        pltpu.make_async_copy(refs[i], refs[count + i], refs[-1].at[i]) for i in range(count)
+    ]
+    for copy in copies:
+        copy.start()
+    for copy in copies:
+        copy.wait()
+
+
 def dense_body(query_proj, key_proj, value_proj, cotangent, boundary, short_taps, skip_gain, long_filter):
     tok, width = query_proj.shape[1:]
     parts = lax.axis_size("seq")
@@ -429,7 +441,7 @@
     f32, bf16 = jnp.float32, jnp.bfloat16
     shape = jax.ShapeDtypeStruct
     dma = pltpu.SemaphoreType.DMA
-    gq, gk, gv, filter_grad, taps_grad, skip_grad = pl.pallas_call(
+    results = pl.pallas_call(
         functools.partial(operator_kernel, n, parts, scale),
         out_shape=[shape((1, tok, width), bf16)] * 3
         + [shape((tok, width), bf16), shape((3, 3, own), f32), shape((1, own), f32)],
@@ -466,8 +478,15 @@
         ),
     )(
         boundary, query_proj, key_proj, value_proj, cotangent, long_filter,
-        short_taps.reshape(9, width), skip_gain[None], jnp.asarray(fine), jnp.asarray(coarse),
-    )
+        short_taps, skip_gain[None], jnp.asarray(fine), jnp.asarray(coarse),
+    )
+    gq, gk, gv, filter_grad, taps_grad, skip_grad = pl.pallas_call(
+        copy_kernel,
+        out_shape=[shape(x.shape, x.dtype) for x in results],
+        in_specs=[anywhere] * len(results),
+        out_specs=[anywhere] * len(results),
+        scratch_shapes=[dma((len(results),))],
+    )(*results)
     return gq, gk, gv, filter_grad, taps_grad, skip_grad.reshape(own)
 
 

time: 114 us -> 171 us (1.50)
  Pallas kernels: 102 us -> 168 us
  local copies, waits for them, and re-layouts: 8.01 us -> 0 us
    pallas_call x0 -> x1, Pallas kernels: none -> 65.1 us  [dense_body(): pl.pallas_call(copy_kernel, out_shape=[shape(x.shape, x.dtype) for x in r...]
    unnamed x16 -> x0, local copies, waits for them, and re-layouts: 6.42 us -> none
where the time goes in v3:
time: 171 us; the launch traced here: 169 us
  Pallas kernels  168 us (98%)
    pallas_call x1, Pallas kernels, dense_body(): pl.pallas_call(functools.partial(operator_kernel, n, parts, scale), out_s...  102 us
    pallas_call x1, Pallas kernels, dense_body(): pl.pallas_call(copy_kernel, out_shape=[shape(x.shape, x.dtype) for x in r...  65.1 us

profile of v3, /device:TPU:0, one launch (start us, length us, event | category | flops | bytes accessed | tf_op | source)
XLA Modules:
  0.0 168.8 jit_solution(3289167695528022021)
XLA Ops:
  1.3 102.4 %shard_map.145 = (bf16[1,128,2048]{2,1,0:T(8,128)(2,1)}, bf16[1,128,2048]{2,1,0:T(8,128)(2,1)}, bf16[1,128,2048]{2,1,0:T(8,128)(2,1)}, bf16[128,2048]{1,0:T(8,12...) custom-call(s32[1]{0:T(128)S(6)} %copy.16.bound, bf16[1,128,2048]{2,1,0:T(8,128)(2,1)} %q_in.1, ...), custom_call_target="tpu_custom_call" | custom-call | tf_op jit(solution)/shard_map/pallas_call | solution.py:444
  103.7 65.1 %shard_map.146 = (bf16[1,128,2048]{2,1,0:T(8,128)(2,1)}, bf16[1,128,2048]{2,1,0:T(8,128)(2,1)}, bf16[1,128,2048]{2,1,0:T(8,128)(2,1)}, bf16[128,2048]{1,0:T(8,12...) custom-call(bf16[1,128,2048]{2,1,0:T(8,128)(2,1)} %get-tuple-element.18.refs_0_, ...), custom_call_target="tpu_custom_call" | custom-call | tf_op jit(solution)/shard_map/pallas_call | solution.py:483

commit v4 on v3

--- a/solution.py
+++ b/solution.py
@@ -144,7 +144,7 @@
 def operator_kernel(
     n, parts, scale, bound, q_in, k_in, v_in, c_in, h_in, taps_in, skip_in, fine, coarse,
     gq_out, gk_out, gv_out, f_out, taps_out, skip_out,
-    bufs, cosines, sines, gd, spec, hspec, gspec, s1s, s2s, dms, ds, filt, fother, fown, stage,
+    hb, bufs, cosines, sines, gd, spec, hspec, gspec, s1s, s2s, dms, ds, filt, fother, fown, stage,
     taps, sums, sother, tsum, send_sem, recv_sem, local_sem, dp_send, dp_recv,
 ):
     tok = n // parts
@@ -154,7 +154,10 @@
     block = min(256, n)
     me = lax.axis_index("seq")
     core = lax.axis_index("dp")
+    group = lax.axis_index("groups")
     partner = {"dp": 1 - core}
+    twin = {"groups": 1 - group}
+    group_rows = pl.ds(pl.multiple_of(group * (tok // 2), tok // 2), tok // 2)
     f32, bf16 = jnp.float32, jnp.bfloat16
     mine = pl.ds(pl.multiple_of(me * tok, tok), tok)
     my_half = pl.ds(pl.multiple_of(core * half, half), half)
@@ -171,8 +174,9 @@
     barrier = pltpu.get_barrier_semaphore()
     for s in range(1, parts):
         pl.semaphore_signal(barrier, inc=1, device_id={"seq": peers[s]}, device_id_type=MESH)
-    pl.semaphore_signal(barrier, inc=1, device_id=partner, device_id_type=MESH)
-    pl.semaphore_wait(barrier, parts)
+    for other in (partner, twin):
+        pl.semaphore_signal(barrier, inc=1, device_id=other, device_id_type=MESH)
+    pl.semaphore_wait(barrier, parts + 1)
 
     def exchange(a, source, target):
         own = pltpu.make_async_copy(source(me), target, local_sem.at[a])
@@ -196,20 +200,22 @@
         for copy in moved[1]:
             copy.wait_recv()
 
-    def to_partner(i, source, target):
+    def to_partner(i, source, target, device=partner):
         return pltpu.make_async_remote_copy(
             src_ref=source,
             dst_ref=target,
             send_sem=dp_send.at[i],
             recv_sem=dp_recv.at[i],
-            device_id=partner,
+            device_id=device,
             device_id_type=MESH,
         )
 
-    hb, kb, vb, qb, cb = (bufs.at[i] for i in range(5))
-    h_moved = exchange(0, lambda o: h_in.at[:, half_cols_of(o)], hb.at[mine, my_half])
+    kb, vb, qb, cb = (bufs.at[i] for i in range(4))
+    h_moved = exchange(
+        0, lambda o: h_in.at[group_rows, half_cols_of(o)], hb.at[me, group, :, my_half]
+    )
     ins = [
-        exchange(1 + i, lambda o, x=x: x.at[0, :, cols_of(o)], bufs.at[1 + i, mine, :])
+        exchange(1 + i, lambda o, x=x: x.at[0, :, cols_of(o)], bufs.at[i, mine, :])
         for i, x in enumerate((k_in, v_in, q_in, c_in))
     ]
 
@@ -281,9 +287,13 @@
         return pl.ds(pl.multiple_of(j * block, block), block)
 
     arrived(h_moved)
-    h_relay = to_partner(0, hb.at[:, my_half], hb.at[:, my_half])
+    h_quarter = hb.at[:, group, :, my_half]
+    h_twin = to_partner(3 + parts, h_quarter, h_quarter, twin)
+    h_twin.start()
+    arrived(ins[0])
+    h_twin.wait_recv()
+    h_relay = to_partner(0, hb.at[:, :, :, my_half], hb.at[:, :, :, my_half])
     h_relay.start()
-    arrived(ins[0])
     arrived(ins[1])
 
     @pl.loop(0, n // rows)
@@ -302,7 +312,7 @@
         at = at_block(j)
         ch, cl = blocks(cosines, at)
         sh, sl = blocks(sines, at)
-        h = hb[...]
+        h = hb[...].reshape(n, width)
         hr, hi = turned(at, dot(ch, h) + dot(cl, h), -(dot(sh, h) + dot(sl, h)))
         hspec[0, at, :], hspec[1, at, :] = hr, hi
         gr, gi = dot3(ch, cl, gd, (0,)), -dot3(sh, sl, gd, (0,))
@@ -358,6 +368,23 @@
     @pl.loop(0, n // block)
     def _(j):
         at = at_block(j)
+        filt[at, :] = inverse(2, at) * (scale / n)
+
+    f_add = to_partner(1, filt.at[:, other_half], fother)
+    f_add.start()
+    f_add.wait_recv()
+
+    @pl.loop(0, n // rows)
+    def _(i):
+        at = at_rows(i)
+        fown[at, :] = (filt[at, my_half] + fother[at, :]).astype(bf16)
+
+    f_moved = exchange(8, lambda o: fown.at[rows_of(o), :], f_out.at[:, half_cols_of(me)])
+    own_relay = to_partner(3, fown.at[mine, :], f_out.at[:, half_cols_of(me)])
+    own_relay.start()
+    @pl.loop(0, n // block)
+    def _(j):
+        at = at_block(j)
         ds[1, at, :] = inverse(1, at) * (1.0 / n)
 
     @pl.loop(0, n // rows)
@@ -372,27 +399,10 @@
     gk_moved = send_back(1, gk_out)
     gv_moved = send_back(2, gv_out)
 
-    @pl.loop(0, n // block)
-    def _(j):
-        at = at_block(j)
-        filt[at, :] = inverse(2, at) * (scale / n)
-
-    f_add = to_partner(1, filt.at[:, other_half], fother)
-    f_add.start()
     sums[...] = jnp.zeros_like(sums)
     sums[pl.ds(0, 10), :] = jnp.sum(tsum[...], axis=1) * scale
     s_add = to_partner(2, sums, sother)
     s_add.start()
-    f_add.wait_recv()
-
-    @pl.loop(0, n // rows)
-    def _(i):
-        at = at_rows(i)
-        fown[at, :] = (filt[at, my_half] + fother[at, :]).astype(bf16)
-
-    f_moved = exchange(8, lambda o: fown.at[rows_of(o), :], f_out.at[:, half_cols_of(me)])
-    own_relay = to_partner(3, fown.at[mine, :], f_out.at[:, half_cols_of(me)])
-    own_relay.start()
     s_add.wait_recv()
     total = sums[...] + sother[...]
     for b in range(3):
@@ -414,19 +424,14 @@
     for moved in (h_moved, *ins, gq_moved, gk_moved, gv_moved, f_moved):
         for copy in moved[1]:
             copy.wait_send()
-    for copy in (h_relay, f_add, s_add, *relays):
+    for copy in (h_twin, h_relay, f_add, s_add, *relays):
         copy.wait_send()
 
 
 def copy_kernel(*refs):
     count = len(refs) // 2
-    copies = [
-        pltpu.make_async_copy(refs[i], refs[count + i], refs[-1].at[i]) for i in range(count)
-    ]
-    for copy in copies:
-        copy.start()
-    for copy in copies:
-        copy.wait()
+    for i in range(count):
+        refs[count + i][...] = refs[i][...]
 
 
 def dense_body(query_proj, key_proj, value_proj, cotangent, boundary, short_taps, skip_gain, long_filter):
@@ -441,6 +446,11 @@
     f32, bf16 = jnp.float32, jnp.bfloat16
     shape = jax.ShapeDtypeStruct
     dma = pltpu.SemaphoreType.DMA
+    blocks = [pl.BlockSpec((1, tok // 4, width), lambda i: (0, i, 0))] * 3 + [
+        pl.BlockSpec((tok // 4, width), lambda i: (i, 0)),
+        pl.BlockSpec((3, 3, own), lambda i: (0, 0, 0)),
+        pl.BlockSpec((1, own), lambda i: (0, 0)),
+    ]
     results = pl.pallas_call(
         functools.partial(operator_kernel, n, parts, scale),
         out_shape=[shape((1, tok, width), bf16)] * 3
@@ -448,7 +458,8 @@
         in_specs=[pl.BlockSpec(memory_space=pltpu.SMEM)] + [anywhere] * 5 + [vmem] * 4,
         out_specs=[anywhere] * 4 + [vmem] * 2,
         scratch_shapes=[
-            pltpu.VMEM((5, n, own), bf16),
+            pltpu.VMEM((parts, 2, tok // 2, own), bf16),
+            pltpu.VMEM((4, n, own), bf16),
             pltpu.VMEM((2, n, n), bf16),
             pltpu.VMEM((2, n, n), bf16),
             pltpu.VMEM((2, 2, n, own), bf16),
@@ -470,8 +481,8 @@
             dma((9, parts)),
             dma((9, parts)),
             dma((9,)),
-            dma((3 + parts,)),
-            dma((3 + parts,)),
+            dma((4 + parts,)),
+            dma((4 + parts,)),
         ],
         compiler_params=pltpu.CompilerParams(
             collective_id=0, has_side_effects=True, vmem_limit_bytes=56 * 2**20
@@ -483,9 +494,9 @@
     gq, gk, gv, filter_grad, taps_grad, skip_grad = pl.pallas_call(
         copy_kernel,
         out_shape=[shape(x.shape, x.dtype) for x in results],
-        in_specs=[anywhere] * len(results),
-        out_specs=[anywhere] * len(results),
-        scratch_shapes=[dma((len(results),))],
+        grid=(4,),
+        in_specs=blocks,
+        out_specs=blocks,
     )(*results)
     return gq, gk, gv, filter_grad, taps_grad, skip_grad.reshape(own)
 
@@ -584,7 +595,7 @@
     )
     def chosen(query_proj, *rest):
         pairs, tok, _ = query_proj.shape
-        dense = pairs == 1 and mesh.shape["dp"] == 2 and tok * mesh.shape["seq"] <= DENSE_LIMIT
+        dense = pairs == 1 and mesh.shape["dp"] == mesh.shape["groups"] == 2 and tok * mesh.shape["seq"] <= DENSE_LIMIT
         return (dense_body if dense else body)(query_proj, *rest)
 
     return jax.shard_map(chosen, mesh=mesh, in_specs=in_specs, out_specs=out_specs, check_vma=False)

time: 171 us -> 104 us (0.61)
  the two profiles are of different devices: /device:TPU:0 before, /device:TPU:31 now
where the time goes in v4:
time: 104 us; the launch traced here: 103 us
  Pallas kernels  102 us (98%)
  between operations  1.29 us (1%)
    pallas_call x1, Pallas kernels, dense_body(): pl.pallas_call(functools.partial(operator_kernel, n, parts, scale), out_s...  98.3 us
    pallas_call x1, Pallas kernels, dense_body(): pl.pallas_call(copy_kernel, out_shape=[shape(x.shape, x.dtype) for x in r...  3.82 us

profile of v4, /device:TPU:31, one launch (start us, length us, event | category | flops | bytes accessed | tf_op | source)
XLA Modules:
  0.0 103.5 jit_solution(12770012028086475300)
XLA Ops:
  1.3 98.3 %shard_map.145 = (bf16[1,128,2048]{2,1,0:T(8,128)(2,1)}, bf16[1,128,2048]{2,1,0:T(8,128)(2,1)}, bf16[1,128,2048]{2,1,0:T(8,128)(2,1)}, bf16[128,2048]{1,0:T(8,12...) custom-call(s32[1]{0:T(128)S(6)} %copy.16.bound, bf16[1,128,2048]{2,1,0:T(8,128)(2,1)} %q_in.1, ...), custom_call_target="tpu_custom_call" | custom-call | tf_op jit(solution)/shard_map/pallas_call | solution.py:454
  99.6 3.8 %shard_map.146 = (bf16[1,128,2048]{2,1,0:T(8,128)(2,1)}, bf16[1,128,2048]{2,1,0:T(8,128)(2,1)}, bf16[1,128,2048]{2,1,0:T(8,128)(2,1)}, bf16[128,2048]{1,0:T(8,12...) custom-call(bf16[1,128,2048]{2,1,0:T(8,128)(2,1)} %get-tuple-element.18.refs_0_, ...), custom_call_target="tpu_custom_call" | custom-call | tf_op jit(solution)/shard_map/pallas_call | solution.py:494
